TPU v7x, 128 devices: a whole 4x4x4 slice. The times are simulated.
128 devices in a mesh: chan: 16 (over x_hi, z, core), tm: 8 (over x_lo, y).
Axes of the slice: x: 4 (x_hi: 2, x_lo: 2; x = x_hi * 2 + x_lo), y: 4, z: 4, core: 2. Of those that a mesh axis runs over, the one named last changes fastest.
Arguments:
- traces: float32 [512, 131072], P('chan', 'tm'), may hold values from -8 to 8
- live_channel: int32 [512], P('chan'), may hold values 0 or 1
- valid_segment: int32 [512, 512], P('chan', 'tm'), may hold values 0 or 1
Outputs:
- correlation: float32 [512, 512, 256], P('chan', 'tm')
All inputs are finite; a program needn't handle non-finite values. No bound on the sum of `live_channel` or of `valid_segment` on one device may be relied on, other than what follows from the above.
Results may differ from a plain program's by a relative error of at most 0.003.
Values may be sent and summed in bfloat16 or wider, within the bound.
No kernel may reach another device: no remote copies, remote signals or barrier semaphores. Data moves between devices by JAX's collectives and lax.ppermute only.
A program may use at most 192 MiB of HBM per device.

v0:
```python
import jax
import jax.numpy as jnp
from jax import lax
from jax.sharding import PartitionSpec as P

SEG_LEN = 256
BINS = 128
HALF_WIN = 64
SMOOTH = 4


def with_halo(array, sides, width):
    for axis, dim in sides:
        count, length = (lax.axis_size(axis), array.shape[dim])
        up = [(i, (i + 1) % count) for i in range(count - 1)]
        down = [(j, i) for i, j in up]
        last = lax.slice_in_dim(array, length - width, length, axis=dim)
        first = lax.slice_in_dim(array, 0, width, axis=dim)
        before = lax.ppermute(last, axis, up)
        after = lax.ppermute(first, axis, down)
        array = jnp.concatenate([before, array, after], axis=dim)
    return array


def make_tables():
    length = SEG_LEN
    times_col = jnp.arange(length, dtype=jnp.int32)[:, None]
    freq_row = jnp.arange(BINS, dtype=jnp.int32)[None, :]
    phase = 2.0 * jnp.pi / length * (times_col * freq_row % length).astype(jnp.float32)
    forward_table = jnp.concatenate([jnp.cos(phase), -jnp.sin(phase)], axis=1)
    freq_col = jnp.arange(BINS, dtype=jnp.int32)[:, None]
    lag_row = jnp.arange(length, dtype=jnp.int32)[None, :] - BINS
    back_phase = 2.0 * jnp.pi / length * (freq_col * lag_row % length).astype(jnp.float32)
    inverse_table = jnp.concatenate([jnp.cos(back_phase), -jnp.sin(back_phase)], axis=0)
    bin_a = jnp.arange(BINS, dtype=jnp.int32)[:, None]
    bin_b = jnp.arange(BINS, dtype=jnp.int32)[None, :]
    smooth_table = (jnp.abs(bin_a - bin_b) <= SMOOTH).astype(jnp.float32) / (2.0 * SMOOTH + 1.0)
    bandpass = (jnp.arange(BINS, dtype=jnp.int32) > 0).astype(jnp.float32)
    sample_in = jnp.arange(SEG_LEN + 2 * HALF_WIN, dtype=jnp.int32)[:, None]
    sample_out = jnp.arange(SEG_LEN, dtype=jnp.int32)[None, :]
    inside = (sample_in >= sample_out) & (sample_in <= sample_out + 2 * HALF_WIN)
    box_table = inside.astype(jnp.float32) / (2.0 * HALF_WIN + 1.0)
    return (forward_table, inverse_table, smooth_table, bandpass, box_table)


def make_accumulate(local_spec, local_mask, pieces):
    spec_block, mask_block = pieces
    turned = jnp.stack([spec_block[:, :, 1], -spec_block[:, :, 0]], axis=2)
    cross_real = jnp.einsum(
        "iscf,jscf->ijf", local_spec, spec_block, preferred_element_type=jnp.float32
    )
    cross_imag = jnp.einsum(
        "iscf,jscf->ijf", local_spec, turned, preferred_element_type=jnp.float32
    )
    block_cross = jnp.stack([cross_real, cross_imag], axis=2)
    block_count = jnp.dot(local_mask, mask_block.T, preferred_element_type=jnp.float32)
    return (block_cross, block_count)


def body(traces, live_channel, valid_segment):
    forward_table, inverse_table, smooth_table, bandpass, box_table = make_tables()
    highest = lax.Precision.HIGHEST
    chan_rows = traces.shape[0]
    seg_count = valid_segment.shape[1]
    span = seg_count * SEG_LEN
    magnitude = jnp.abs(traces)
    slab_ends = jnp.concatenate([magnitude[:, :HALF_WIN], magnitude[:, span - HALF_WIN :]], axis=1)
    rims = with_halo(slab_ends, (("tm", 1),), HALF_WIN)
    padded = jnp.concatenate(
        [rims[:, :HALF_WIN], magnitude, rims[:, rims.shape[1] - HALF_WIN :]], axis=1
    )
    head_part = padded[:, :span].reshape(chan_rows, seg_count, SEG_LEN)
    extended = jnp.pad(padded, ((0, 0), (0, SEG_LEN - 2 * HALF_WIN)))
    tail_part = extended[:, SEG_LEN : SEG_LEN + span].reshape(chan_rows, seg_count, SEG_LEN)[
        :, :, : 2 * HALF_WIN
    ]
    window = jnp.concatenate([head_part, tail_part], axis=2)
    abs_level = jnp.dot(window, box_table, precision=highest, preferred_element_type=jnp.float32)
    normed = traces.reshape(chan_rows, seg_count, SEG_LEN) / (abs_level + 1e-05)
    spectrum = jnp.dot(normed, forward_table, precision=highest, preferred_element_type=jnp.float32)
    spectrum = spectrum.reshape(chan_rows, seg_count, 2, BINS)
    spectral_power = spectrum[:, :, 0] ** 2 + spectrum[:, :, 1] ** 2
    smoothed = jnp.dot(
        spectral_power, smooth_table, precision=highest, preferred_element_type=jnp.float32
    )
    mean_power = jnp.mean(spectral_power, axis=-1, keepdims=True)
    seg_mask = (live_channel[:, None] * valid_segment).astype(jnp.bfloat16)
    whiten_scale = (
        bandpass
        * seg_mask.astype(jnp.float32)[:, :, None]
        / jnp.sqrt(smoothed + 0.1 * mean_power + 1e-06)
    )
    whitened = (spectrum * whiten_scale[:, :, None, :]).astype(jnp.bfloat16)
    cross_all, count_all = make_accumulate(
        whitened,
        seg_mask,
        (
            lax.all_gather(whitened, "chan", axis=0, tiled=True),
            lax.all_gather(seg_mask, "chan", axis=0, tiled=True),
        ),
    )
    cross_mine, count_mine = (
        lax.psum_scatter(cross_all, "tm", scatter_dimension=1, tiled=True),
        lax.psum_scatter(count_all, "tm", scatter_dimension=1, tiled=True),
    )
    col_count = cross_mine.shape[1]
    flat_cross = cross_mine.reshape(chan_rows, col_count, 2 * BINS)
    lagged = jnp.dot(
        flat_cross, inverse_table, precision=highest, preferred_element_type=jnp.float32
    )
    return lagged * (2.0 / jnp.maximum(count_mine, 1.0))[:, :, None]


def solution(mesh):
    return jax.shard_map(
        body,
        mesh=mesh,
        in_specs=(P("chan", "tm"), P("chan"), P("chan", "tm")),
        out_specs=P("chan", "tm", None),
        check_vma=False,
    )
```

profile of v0, /device:TPU:1, one launch (start us, length us, event | category | flops | bytes accessed | tf_op | source)
XLA Modules:
  0.0 535.7 jit_solution(15726900445165591918)
XLA Ops:
  7.4 1.9 abs.6
  9.4 4.0 collective-permute-start
  13.4 1.3 collective-permute-start.1
  15.4 2.0 copy.30
  17.9 2.4 concatenate.16
  20.3 1.7 pad_slice_fusion
  24.9 3.9 bitcast_divide_fusion
  28.9 3.1 fusion.22
  32.0 2.3 reshape.44
  34.3 3.5 copy.19
  37.8 2.3 fusion.60
  41.5 1.8 copy.18
  43.4 4.6 multiply_convert_fusion
  48.0 27.9 %all_gather.7 = bf16[512,64]{1,0:T(8,128)(2,1)S(1)} all-gather(bf16[32,64]{1,0:T(8,128)(2,1)S(1)} %get-tuple-element.6), channel_id=1, replica_groups=mesh['chan'=16,'tm'=8] {'chan'}, dimensions={0}, use_global_device_ids=true | all-gather | bytes 69632 | tf_op jit(solution)/shard_map/all_gather | solution.py:99
  76.8 180.3 %all-gather.2.cloned.1.call-done = bf16[512,64,2,128]{1,0,2,3:T(8,128)(2,1)} async-done(((bf16[32,64,2,128]{1,0,2,3:T(8,128)(2,1)}), bf16[512,64,2,128]{1,0,2,3:T(8,128)(2,1)}) %all-gather.2.cloned.1.call-update) | async-done | bytes 16777232 | tf_op jit(solution)/shard_map/all_gather | solution.py:98
  257.1 23.0 %fusion.59 = (bf16[512,64,1,128]{1,0,2,3:T(8,128)(2,1)}, bf16[512,64,1,128]{1,0,2,3:T(8,128)(2,1)}) fusion(bf16[512,64,2,128]{1,0,2,3:T(8,128)(2,1)} %all-gather.2.cloned.1.call-done), kind=kLoop, calls=%fused_computation.84 | loop fusion | flops 4194304 | bytes 33554432 | tf_op jit(solution)/shard_map/slice | solution.py:48
  280.1 17.7 %fusion.4 = f32[32,512,1,128]{1,0,3,2:T(8,128)} fusion(bf16[32,64,2,128]{1,0,2,3:T(8,128)(2,1)S(1)} %copy-done, bf16[512,64,1,128]{1,0,2,3:T(8,128)(2,1)} %get-tuple-element.8, bf16[512,64,1,128]{1,0,2,3:T(8,128)(2,1)} %get-tuple-element.7), kind=kOutput, calls=%fused_computation.7 | convolution fusion | flops 545259520 | bytes 26214400 | tf_op jit(solution)/shard_map/iscf,jscf->ijf/dot_general | solution.py:52
  297.8 18.5 %convolution_bitcast_fusion = f32[32,512,1,128]{1,0,3,2:T(8,128)} fusion(bf16[512,64,2,128]{1,0,2,3:T(8,128)(2,1)} %all-gather.2.cloned.1.call-done, bf16[32,64,2,128]{1,0,2,3:T(8,128)(2,1)S(1)} %copy-done), kind=kOutput, calls=%fused_computation.8 | convolution fusion | flops 536870912 | bytes 26214400 | tf_op jit(solution)/shard_map/iscf,jscf->ijf/dot_general | solution.py:49
  316.4 12.3 %pad_maximum_fusion = f32[32,512,2,128]{1,0,3,2:T(8,128)} fusion(f32[32,512,1,128]{1,0,3,2:T(8,128)} %fusion.4, f32[32,512,1,128]{1,0,3,2:T(8,128)} %convolution_bitcast_fusion), kind=kLoop, calls=%fused_computation.5 | loop fusion | flops 4194304 | bytes 33554432 | tf_op jit(solution)/shard_map/stack | solution.py:55
  328.6 21.1 %copy.21 = f32[32,512,2,128]{3,0,2,1:T(8,128)} copy(f32[32,512,2,128]{1,0,3,2:T(8,128)} %pad_maximum_fusion) | data formatting | bytes 33554432 | tf_op jit(solution)/shard_map/stack | solution.py:55
  351.2 166.5 %reduce-scatter.5.cloned.1.call-done = f32[32,64,2,128]{3,0,2,1:T(8,128)} async-done(((f32[32,512,2,128]{3,0,2,1:T(8,128)}), f32[32,64,2,128]{3,0,2,1:T(8,128)}) %reduce-scatter.5.cloned.1.call-update) | async-done | bytes 2097168 | tf_op jit(solution)/shard_map/reduce_scatter | solution.py:103
  517.7 4.5 copy.22
  522.2 2.9 reshape.45
  525.1 3.1 convolution_multiply_fusion
  (36 shorter events, 8.0 us)
Async XLA Ops:
  7.4 7.9 %copy-start.3 = (s32[32,64]{1,0:T(8,128)S(1)}, s32[32,64]{1,0:T(8,128)}, u32[]{:S(2)}) copy-start(s32[32,64]{1,0:T(8,128)} %param.5) | copy-start | bytes 24580
  7.4 7.9 %copy-start.4 = (s32[32]{0:T(128)S(1)}, s32[32]{0:T(128)}, u32[]{:S(2)}) copy-start(s32[32]{0:T(128)} %param.4) | copy-start | bytes 388
  7.4 249.7 %all-gather.2.cloned.1.call-start = ((), (), s32[]{:S(2)}) async-start(), calls=%async_computation.2 | async-start | bytes 35651584 | tf_op jit(solution)/shard_map/all_gather | solution.py:98
  7.4 8.0 %copy-start.1 = (f32[32,16384]{1,0:T(8,128)S(1)}, f32[32,16384]{1,0:T(8,128)}, u32[]{:S(2)}) copy-start(f32[32,16384]{1,0:T(8,128)} %param.3) | copy-start | bytes 6291460
  9.4 7.9 %collective-permute-start = (f32[32,64]{1,0:T(8,128)S(1)}, f32[32,64]{1,0:T(8,128)S(1)}, u32[]{:S(2)}, u32[]{:S(2)}) collective-permute-start(f32[32,64]{1,0:T(8,128)S(1)} %get-tuple-element.12), channel_id=1, source_target_pairs={{0,1},{1,2},{2,3},{3,4},{4,5},{5,6},{6,7},{8,9},{9,10},{10,11},{11... | collective-permute-start | bytes 24584 | tf_op jit(solution)/shard_map/ppermute | solution.py:19
  13.4 4.5 collective-permute-start.1
  23.3 1.6 copy-start.2
  47.9 302.4 %reduce-scatter.7.cloned.1.call-start = ((), (), s32[]{:S(2)}) async-start(), calls=%async_computation.4 | async-start | bytes 294912
  76.7 203.4 %copy-start = (bf16[32,64,2,128]{1,0,2,3:T(8,128)(2,1)S(1)}, bf16[32,64,2,128]{1,0,2,3:T(8,128)(2,1)}, u32[]{:S(2)}) copy-start(bf16[32,64,2,128]{1,0,2,3:T(8,128)(2,1)} %multiply_convert_fusion) | copy-start | bytes 3145732
  76.7 440.9 %reduce-scatter.5.cloned.1.call-start = ((), (), s32[]{:S(2)}) async-start(), calls=%async_computation.3 | async-start | bytes 18874368 | tf_op jit(solution)/shard_map/reduce_scatter | solution.py:103
Sparse Core Ops, SparseCore 0:
  48.1 209.0 all-gather.1
Sparse Core Ops, SparseCore 1:
  76.8 34.0 reduce-scatter.6
  349.8 167.8 reduce-scatter.4
where the time goes:
time: 537 us; the launch traced here: 536 us
  waiting for transfers between devices  347 us (65%)
  matrix products  48.4 us (9%)
  local copies, waits for them, and re-layouts  47.7 us (9%)
  other arithmetic  43.9 us (8%)
  blocking collectives  27.9 us (5%)
  between operations  15 us (3%)
  starting transfers between devices  5.4 us (1%)
    all_gather x1, waiting for transfers between devices, body(): lax.all_gather(whitened, 'chan', axis=0, tiled=True)  180 us
    reduce_scatter x1, waiting for transfers between devices, body(): lax.psum_scatter(cross_all, 'tm', scatter_dimension=1, tiled=True)  167 us
    all_gather x1, blocking collectives, body(): lax.all_gather(seg_mask, 'chan', axis=0, tiled=True)  27.9 us
    slice x1, other arithmetic, make_accumulate(): turned = jnp.stack([spec_block[:, :, 1], -spec_block[:, :, 0]], axis=2)  23 us
    another operation x1, local copies, waits for them, and re-layouts, make_accumulate(): block_cross = jnp.stack([cross_real, cross_imag], axis=2)  21.1 us
    dot_general x1, matrix products, make_accumulate(): jnp.einsum('iscf,jscf->ijf', local_spec, spec_block, preferred_element_ty...  18.5 us
    dot_general x1, matrix products, make_accumulate(): jnp.einsum('iscf,jscf->ijf', local_spec, turned, preferred_element_type=j...  17.7 us
    another operation x1, other arithmetic, make_accumulate(): block_cross = jnp.stack([cross_real, cross_imag], axis=2)  12.3 us
  transfers between devices with their start and end apart: 5, of which 3 were waited for; matrix products, arithmetic and copies ran while one was open for 18% of the time, Pallas kernels for 0%

commit v1 on v0

--- a/solution.py
+++ b/solution.py
@@ -7,6 +7,7 @@
 BINS = 128
 HALF_WIN = 64
 SMOOTH = 4
+ALL = ("chan", "tm")
 
 
 def with_halo(array, sides, width):
@@ -31,30 +32,17 @@
     freq_col = jnp.arange(BINS, dtype=jnp.int32)[:, None]
     lag_row = jnp.arange(length, dtype=jnp.int32)[None, :] - BINS
     back_phase = 2.0 * jnp.pi / length * (freq_col * lag_row % length).astype(jnp.float32)
-    inverse_table = jnp.concatenate([jnp.cos(back_phase), -jnp.sin(back_phase)], axis=0)
+    bandpass = (jnp.arange(BINS, dtype=jnp.int32) > 0).astype(jnp.float32)
+    inverse_table = jnp.stack([jnp.cos(back_phase), -jnp.sin(back_phase)], axis=1)
+    inverse_table = inverse_table * bandpass[:, None, None]
     bin_a = jnp.arange(BINS, dtype=jnp.int32)[:, None]
     bin_b = jnp.arange(BINS, dtype=jnp.int32)[None, :]
     smooth_table = (jnp.abs(bin_a - bin_b) <= SMOOTH).astype(jnp.float32) / (2.0 * SMOOTH + 1.0)
-    bandpass = (jnp.arange(BINS, dtype=jnp.int32) > 0).astype(jnp.float32)
     sample_in = jnp.arange(SEG_LEN + 2 * HALF_WIN, dtype=jnp.int32)[:, None]
     sample_out = jnp.arange(SEG_LEN, dtype=jnp.int32)[None, :]
     inside = (sample_in >= sample_out) & (sample_in <= sample_out + 2 * HALF_WIN)
     box_table = inside.astype(jnp.float32) / (2.0 * HALF_WIN + 1.0)
     return (forward_table, inverse_table, smooth_table, bandpass, box_table)
-
-
-def make_accumulate(local_spec, local_mask, pieces):
-    spec_block, mask_block = pieces
-    turned = jnp.stack([spec_block[:, :, 1], -spec_block[:, :, 0]], axis=2)
-    cross_real = jnp.einsum(
-        "iscf,jscf->ijf", local_spec, spec_block, preferred_element_type=jnp.float32
-    )
-    cross_imag = jnp.einsum(
-        "iscf,jscf->ijf", local_spec, turned, preferred_element_type=jnp.float32
-    )
-    block_cross = jnp.stack([cross_real, cross_imag], axis=2)
-    block_count = jnp.dot(local_mask, mask_block.T, preferred_element_type=jnp.float32)
-    return (block_cross, block_count)
 
 
 def body(traces, live_channel, valid_segment):
@@ -63,6 +51,7 @@
     chan_rows = traces.shape[0]
     seg_count = valid_segment.shape[1]
     span = seg_count * SEG_LEN
+    chans, slabs = lax.axis_size("chan"), lax.axis_size("tm")
     magnitude = jnp.abs(traces)
     slab_ends = jnp.concatenate([magnitude[:, :HALF_WIN], magnitude[:, span - HALF_WIN :]], axis=1)
     rims = with_halo(slab_ends, (("tm", 1),), HALF_WIN)
@@ -84,31 +73,37 @@
         spectral_power, smooth_table, precision=highest, preferred_element_type=jnp.float32
     )
     mean_power = jnp.mean(spectral_power, axis=-1, keepdims=True)
-    seg_mask = (live_channel[:, None] * valid_segment).astype(jnp.bfloat16)
+    seg_mask = (live_channel[:, None] * valid_segment).astype(jnp.float32)
     whiten_scale = (
-        bandpass
-        * seg_mask.astype(jnp.float32)[:, :, None]
-        / jnp.sqrt(smoothed + 0.1 * mean_power + 1e-06)
+        bandpass * seg_mask[:, :, None] / jnp.sqrt(smoothed + 0.1 * mean_power + 1e-06)
     )
-    whitened = (spectrum * whiten_scale[:, :, None, :]).astype(jnp.bfloat16)
-    cross_all, count_all = make_accumulate(
-        whitened,
-        seg_mask,
-        (
-            lax.all_gather(whitened, "chan", axis=0, tiled=True),
-            lax.all_gather(seg_mask, "chan", axis=0, tiled=True),
-        ),
+    whitened = spectrum * whiten_scale[:, :, None, :]
+    carries = jnp.zeros((2, BINS), jnp.float32).at[0, 0].set(1.0)
+    whitened = (whitened + seg_mask[:, :, None, None] * carries).astype(jnp.bfloat16)
+    sent = jnp.transpose(whitened, (3, 0, 2, 1)).reshape(BINS, chan_rows, 2 * seg_count)
+    got = lax.all_to_all(sent, ALL, 0, 0, tiled=True)
+    got = got.reshape(chans, slabs, chan_rows, 2, seg_count)
+    spec = jnp.transpose(got, (0, 2, 1, 3, 4)).reshape(chans * chan_rows, slabs, 2, seg_count)
+    turned = jnp.stack([spec[:, :, 1], -spec[:, :, 0]], axis=2)
+    flat = spec.reshape(chans * chan_rows, -1)
+    cross_real = jnp.dot(flat, flat.T, preferred_element_type=jnp.float32)
+    cross_imag = jnp.dot(
+        flat, turned.reshape(chans * chan_rows, -1).T, preferred_element_type=jnp.float32
     )
-    cross_mine, count_mine = (
-        lax.psum_scatter(cross_all, "tm", scatter_dimension=1, tiled=True),
-        lax.psum_scatter(count_all, "tm", scatter_dimension=1, tiled=True),
+    rounded = lax.reduce_precision(cross_real, 8, 7)
+    is_count = (lax.axis_index(ALL) == 0)
+    cross_imag = jnp.where(is_count, cross_real - rounded, cross_imag)
+    cols = (chans * chan_rows) // slabs
+    pieces = jnp.stack([rounded, cross_imag], axis=0).astype(jnp.bfloat16)
+    pieces = pieces.reshape(2, chans, chan_rows, slabs, cols)
+    pieces = jnp.transpose(pieces, (1, 3, 2, 0, 4)).reshape(BINS, chan_rows, 2 * cols)
+    back = lax.all_to_all(pieces, ALL, 0, 0, tiled=True)
+    back = back.reshape(BINS, chan_rows, 2, cols).astype(jnp.float32)
+    count = back[0, :, 0] + back[0, :, 1]
+    lagged = jnp.einsum(
+        "fikj,fkl->ijl", back, inverse_table, precision=highest, preferred_element_type=jnp.float32
     )
-    col_count = cross_mine.shape[1]
-    flat_cross = cross_mine.reshape(chan_rows, col_count, 2 * BINS)
-    lagged = jnp.dot(
-        flat_cross, inverse_table, precision=highest, preferred_element_type=jnp.float32
-    )
-    return lagged * (2.0 / jnp.maximum(count_mine, 1.0))[:, :, None]
+    return lagged * (2.0 / jnp.maximum(count, 1.0))[:, :, None]
 
 
 def solution(mesh):

time: 537 us -> 128 us (0.24)
  waiting for transfers between devices: 347 us -> 37.8 us
  matrix products: 48.4 us -> 11.5 us
  other arithmetic: 43.9 us -> 13.6 us
  blocking collectives: 27.9 us -> 0 us
  starting transfers between devices: 5.4 us -> 23.3 us
  between operations: 15 us -> 0.29 us
  local copies, waits for them, and re-layouts: 47.7 us -> 41.2 us
    all_gather x1 -> x0, waiting for transfers between devices: 180 us -> none  [body(): lax.all_gather(whitened, 'chan', axis=0, tiled=True)]
    reduce_scatter x1 -> x0, waiting for transfers between devices: 167 us -> none  [body(): lax.psum_scatter(cross_all, 'tm', scatter_dimension=1, tiled=True)]
    all_to_all x0 -> x2, waiting for transfers between devices: none -> 37.2 us  [the longest x1 18.8 us: body(): got = lax.all_to_all(sent, ALL, 0, 0, tiled=True)]
    dot_general x3, matrix products: 39.4 us -> 4.65 us  [the longest x1 2.4 us: body(): jnp.einsum('fikj,fkl->ijl', back, inverse_table, precision=highest, prefe...]
    all_gather x1 -> x0, blocking collectives: 27.9 us -> none  [body(): lax.all_gather(seg_mask, 'chan', axis=0, tiled=True)]
    slice x1, other arithmetic: 23 us -> 0.27 us  [body(): turned = jnp.stack([spec[:, :, 1], -spec[:, :, 0]], axis=2)]
    all_to_all x0 -> x2, starting transfers between devices: none -> 18 us  [the longest x1 13.3 us: body(): got = lax.all_to_all(sent, ALL, 0, 0, tiled=True)]
    another operation x1, other arithmetic: 12.3 us -> 1.8 us  [body(): turned = jnp.stack([spec[:, :, 1], -spec[:, :, 0]], axis=2)]
  transfers between devices with their start and end apart: 5 -> 4, of which waited for: 3 -> 3; matrix products, arithmetic and copies ran while one was open for 18% -> 2% of each run, Pallas kernels for 0% -> 0%
where the time goes in v1:
time: 128 us
  local copies, waits for them, and re-layouts  41.2 us (32%)
  waiting for transfers between devices  37.8 us (30%)
  starting transfers between devices  23.3 us (18%)
  other arithmetic  13.6 us (11%)
  matrix products  11.5 us (9%)
    all_to_all x1, waiting for transfers between devices, body(): got = lax.all_to_all(sent, ALL, 0, 0, tiled=True)  18.8 us
    all_to_all x1, waiting for transfers between devices, body(): back = lax.all_to_all(pieces, ALL, 0, 0, tiled=True)  18.4 us
    all_to_all x1, starting transfers between devices, body(): got = lax.all_to_all(sent, ALL, 0, 0, tiled=True)  13.3 us
    another operation x4, local copies, waits for them, and re-layouts, body(): pieces = jnp.stack([rounded, cross_imag], axis=0).astype(jnp.bfloat16)  6.86 us
    transpose x1, other arithmetic, body(): jnp.transpose(pieces, (1, 3, 2, 0, 4)).reshape(BINS, chan_rows, 2 * cols)  6.36 us
    transpose x2, local copies, waits for them, and re-layouts, body(): jnp.transpose(got, (0, 2, 1, 3, 4))  6.24 us
    reshape x1, local copies, waits for them, and re-layouts, body(): jnp.transpose(pieces, (1, 3, 2, 0, 4)).reshape(BINS, chan_rows, 2 * cols)  4.75 us
    all_to_all x1, starting transfers between devices, body(): back = lax.all_to_all(pieces, ALL, 0, 0, tiled=True)  4.69 us
  transfers between devices with their start and end apart: 4, of which 3 were waited for; matrix products, arithmetic and copies ran while one was open for 2% of the time, Pallas kernels for 0%

profile of v1, /device:TPU:1, one launch (start us, length us, event | category | flops | bytes accessed | tf_op | source)
XLA Modules:
  0.0 127.6 jit_solution(6622329314948308975)
XLA Ops:
  0.0 1.9 %abs.6 = f32[32,16384]{1,0:T(8,128)S(1)} abs(f32[32,16384]{1,0:T(8,128)} %param.5) | non-fusion elementwise | flops 524288 | bytes 4194304 | tf_op jit(solution)/shard_map/abs | solution.py:55
  2.0 4.0 %collective-permute-start = (f32[32,64]{1,0:T(8,128)S(1)}, f32[32,64]{1,0:T(8,128)S(1)}, u32[]{:S(2)}, u32[]{:S(2)}) collective-permute-start(f32[32,64]{1,0:T(8,128)S(1)} %get-tuple-element.22), channel_id=1, source_target_pairs={{0,1},{1,2},{2,3},{3,4},{4,5},{5,6},{6,7},{8,9},{9,10},{10,11},{11... | collective-permute-start | bytes 24584 | tf_op jit(solution)/shard_map/ppermute | solution.py:20
  8.0 2.0 %copy.39 = f32[4,8,64,256]{3,2,1,0:T(8,128)} copy(f32[4,8,64,256]{3,1,2,0:T(8,128)S(1)} %bitcast.59) | data formatting | bytes 4194304
  10.5 2.4 %concatenate.17 = f32[32,16512]{1,0:T(8,128)} concatenate(f32[32,64]{1,0:T(8,128)S(1)} %collective-permute-done, f32[32,16384]{1,0:T(8,128)S(1)} %abs.6, f32[32,64]{1,0:T(8,128)S(1)} %collective-permute-done.1), dimensions={1} | concatenate | bytes 4227072 | tf_op jit(solution)/shard_map/concatenate | solution.py:58
  12.9 1.7 %pad_slice_fusion = f32[32,16384]{1,0:T(8,128)S(1)} fusion(f32[32,16512]{1,0:T(8,128)} %concatenate.17), kind=kLoop, calls=%fused_computation.4 | loop fusion | bytes 4210688 | tf_op jit(solution)/shard_map/slice | solution.py:63
  17.6 3.9 %bitcast_divide_fusion = f32[32,64,256]{2,1,0:T(8,128)S(1)} fusion(f32[4,8,64,256]{3,2,1,0:T(8,128)S(1)} %copy-done.2, f32[32,64,128]{2,1,0:T(8,128)S(1)} %slice.63, f32[32,64,256]{2,1,0:T(8,128)S(1)} %bitcast.65, s32[256]{0:T(256)S(1)} %iota_add_fusion.1), kind=kOutput, calls=%fused_computation.5 | convolution fusion | flops 2418147328 | bytes 7341056 | tf_op jit(solution)/shard_map/dot_general | solution.py:67
  21.5 1.8 %fusion.21 = f32[32,64,256]{2,1,0:T(8,128)S(1)} fusion(f32[32,64,256]{2,1,0:T(8,128)S(1)} %bitcast_divide_fusion, f32[256,128]{1,0:T(8,128)S(1)} %get-tuple-element.27, f32[256,128]{1,0:T(8,128)S(1)} %get-tuple-element.28), kind=kOutput, calls=%fused_computation.35 | convolution fusion | flops 1610678272 | bytes 4456448 | tf_op jit(solution)/shard_map/dot_general | solution.py:69
  23.3 2.1 %reshape.218 = f32[32,64,2,128]{3,2,1,0:T(2,128)} reshape(f32[32,64,256]{2,1,0:T(8,128)S(1)} %fusion.21) | data formatting | bytes 4194304 | tf_op jit(solution)/shard_map/reshape | solution.py:70
  25.4 4.4 %fusion.60 = (f32[32,64,1,128]{3,2,1,0:T(1,128)S(1)}, f32[32,64,1,128]{3,2,1,0:T(1,128)S(1)}) fusion(f32[32,64,2,128]{3,2,1,0:T(2,128)} %reshape.218), kind=kLoop, calls=%fused_computation.89 | loop fusion | bytes 4194304 | tf_op jit(solution)/shard_map/slice | solution.py:71
  31.8 1.7 %copy.28 = bf16[128,32,128]{2,1,0:T(8,128)(2,1)} copy(bf16[128,32,128]{0,2,1:T(8,128)(2,1)S(1)} %bitcast.64) | data formatting | bytes 2097152 | tf_op jit(solution)/shard_map/reshape | solution.py:83
  33.5 13.3 %all-to-all-start = ((bf16[128,32,128]{2,1,0:T(8,128)(2,1)}), bf16[128,32,128]{2,1,0:T(8,128)(2,1)S(1)}, u32[]{:S(2)}, u32[]{:S(2)}) async-start(bf16[128,32,128]{2,1,0:T(8,128)(2,1)} %copy.28), calls=%async_computation | async-start | bytes 2097152 | tf_op jit(solution)/shard_map/all_to_all | solution.py:84
  46.8 18.8 %all-to-all-done = bf16[128,32,128]{2,1,0:T(8,128)(2,1)S(1)} async-done(((bf16[128,32,128]{2,1,0:T(8,128)(2,1)}), bf16[128,32,128]{2,1,0:T(8,128)(2,1)S(1)}, u32[]{:S(2)}, u32[]{:S(2)}) %all-to-all-start) | async-done | bytes 1048608 | tf_op jit(solution)/shard_map/all_to_all | solution.py:84
  66.4 3.3 %copy.30 = bf16[16,32,8,2,64]{4,2,3,1,0:T(8,128)(2,1)S(1)} copy(bf16[16,32,8,2,64]{4,3,1,2,0:T(2,128)(2,1)S(1)} %bitcast.52) | data formatting | bytes 2097152 | tf_op jit(solution)/shard_map/transpose | solution.py:86
  69.8 2.9 %copy.29 = bf16[16,32,8,2,64]{4,3,2,1,0:T(2,128)(2,1)} copy(bf16[16,32,8,2,64]{4,3,1,2,0:T(2,128)(2,1)S(1)} %bitcast.53) | data formatting | bytes 2097152 | tf_op jit(solution)/shard_map/transpose | solution.py:86
  73.0 1.8 %pad_maximum_fusion.1 = bf16[512,8,2,64]{3,1,2,0:T(8,128)(2,1)} fusion(bf16[512,8,1,64]{3,1,2,0:T(8,128)(2,1)S(1)} %get-tuple-element.18, bf16[512,8,1,64]{3,1,2,0:T(8,128)(2,1)S(1)} %get-tuple-element.17), kind=kLoop, calls=%fused_computation.10 | loop fusion | flops 524288 | bytes 2097152 | tf_op jit(solution)/shard_map/stack | solution.py:87
  74.8 3.4 %copy.31 = bf16[512,8,2,64]{0,3,2,1:T(8,128)(2,1)} copy(bf16[512,8,2,64]{3,1,2,0:T(8,128)(2,1)} %pad_maximum_fusion.1) | data formatting | bytes 2097152 | tf_op jit(solution)/shard_map/stack | solution.py:87
  82.5 2.2 %copy.33 = bf16[1,16,32,8,64]{4,0,2,3,1:T(2,128)(2,1)S(1)} copy(bf16[1,16,32,8,64]{4,3,2,1,0:T(8,128)(2,1)S(1)} %stack.20) | data formatting | bytes 1048576 | tf_op jit(solution)/shard_map/stack | solution.py:97
  84.7 1.9 %stack.18 = bf16[1,16,32,8,64]{4,3,2,1,0:T(8,128)(2,1)S(1)} reshape(bf16[512,512]{1,0:T(8,128)(2,1)} %get-tuple-element.25) | data formatting | bytes 1048576 | tf_op jit(solution)/shard_map/stack | solution.py:97
  86.6 2.2 %copy.32 = bf16[1,16,32,8,64]{4,0,2,3,1:T(2,128)(2,1)S(1)} copy(bf16[1,16,32,8,64]{4,3,2,1,0:T(8,128)(2,1)S(1)} %stack.18) | data formatting | bytes 1048576 | tf_op jit(solution)/shard_map/stack | solution.py:97
  88.8 6.4 %maximum_bitcast_fusion = bf16[16,8,32,2,64]{4,3,2,1,0:T(2,128)(2,1)} fusion(bf16[1,16,32,8,64]{4,0,2,3,1:T(2,128)(2,1)S(1)} %copy.33, bf16[1,16,32,8,64]{4,0,2,3,1:T(2,128)(2,1)S(1)} %copy.32), kind=kLoop, calls=%fused_computation.11 | loop fusion | flops 2097152 | bytes 2097152 | tf_op jit(solution)/shard_map/transpose | solution.py:99
  95.2 4.7 %reshape.223 = bf16[128,32,128]{2,1,0:T(8,128)(2,1)} reshape(bf16[16,8,32,2,64]{4,3,2,1,0:T(2,128)(2,1)} %maximum_bitcast_fusion) | data formatting | bytes 2097152 | tf_op jit(solution)/shard_map/reshape | solution.py:99
  99.9 4.7 %all-to-all-start.1 = ((bf16[128,32,128]{2,1,0:T(8,128)(2,1)}), bf16[128,32,128]{2,1,0:T(8,128)(2,1)S(1)}, u32[]{:S(2)}, u32[]{:S(2)}) async-start(bf16[128,32,128]{2,1,0:T(8,128)(2,1)} %reshape.223), calls=%async_computation.1 | async-start | bytes 2097152 | tf_op jit(solution)/shard_map/all_to_all | solution.py:100
  105.2 18.4 %all-to-all-done.1 = bf16[128,32,128]{2,1,0:T(8,128)(2,1)S(1)} async-done(((bf16[128,32,128]{2,1,0:T(8,128)(2,1)}), bf16[128,32,128]{2,1,0:T(8,128)(2,1)S(1)}, u32[]{:S(2)}, u32[]{:S(2)}) %all-to-all-start.1) | async-done | bytes 1048608 | tf_op jit(solution)/shard_map/all_to_all | solution.py:100
  125.2 2.4 %bitcast_multiply_fusion.1 = f32[32,64,256]{2,1,0:T(8,128)} fusion(bf16[128,32,2,64]{0,3,2,1:T(8,128)(2,1)S(1)} %bitcast.54, f32[32,64]{1,0:T(8,128)S(1)} %fusion.15, f32[128,1,256]{2,0,1:T(8,128)S(1)} %get-tuple-element.24, f32[128,1,256]{2,0,1:T(8,128)S(1)} %get-tuple-element.23, f32[128]{0:T(128)S(1)} %compare_convert_fusion), kind=kOutput, calls=%fused_computation.12 | convolution fusion | flops 1611268096 | bytes 3416576 | tf_op jit(solution)/shard_map/fikj,fkl->ijl/dot_general | solution.py:103
  (41 shorter events, 14.9 us)
Async XLA Ops:
  0.0 8.0 %copy-start = (f32[32,16384]{1,0:T(8,128)S(1)}, f32[32,16384]{1,0:T(8,128)}, u32[]{:S(2)}) copy-start(f32[32,16384]{1,0:T(8,128)} %param.5) | copy-start | bytes 6291460
  0.0 7.9 %copy-start.6 = (s32[32]{0:T(128)S(1)}, s32[32]{0:T(128)}, u32[]{:S(2)}) copy-start(s32[32]{0:T(128)} %param.6) | copy-start | bytes 388
  0.0 7.9 %copy-start.4 = (s32[32,64]{1,0:T(8,128)S(1)}, s32[32,64]{1,0:T(8,128)}, u32[]{:S(2)}) copy-start(s32[32,64]{1,0:T(8,128)} %param.7) | copy-start | bytes 24580
  2.0 7.9 %collective-permute-start = (f32[32,64]{1,0:T(8,128)S(1)}, f32[32,64]{1,0:T(8,128)S(1)}, u32[]{:S(2)}, u32[]{:S(2)}) collective-permute-start(f32[32,64]{1,0:T(8,128)S(1)} %get-tuple-element.22), channel_id=1, source_target_pairs={{0,1},{1,2},{2,3},{3,4},{4,5},{5,6},{6,7},{8,9},{9,10},{10,11},{11... | collective-permute-start | bytes 24584 | tf_op jit(solution)/shard_map/ppermute | solution.py:20
  6.0 4.5 %collective-permute-start.1 = (f32[32,64]{1,0:T(8,128)S(1)}, f32[32,64]{1,0:T(8,128)S(1)}, u32[]{:S(2)}, u32[]{:S(2)}) collective-permute-start(f32[32,64]{1,0:T(8,128)S(1)} %get-tuple-element.21), channel_id=1, source_target_pairs={{1,0},{2,1},{3,2},{4,3},{5,4},{6,5},{7,6},{9,8},{10,9},{11,10},{12... | collective-permute-start | bytes 24584 | tf_op jit(solution)/shard_map/ppermute | solution.py:21
  16.0 1.6 %copy-start.2 = (f32[4,8,64,256]{3,2,1,0:T(8,128)S(1)}, f32[4,8,64,256]{3,2,1,0:T(8,128)}, u32[]{:S(2)}) copy-start(f32[4,8,64,256]{3,2,1,0:T(8,128)} %copy.39) | copy-start | bytes 6291460
  30.2 1.1 copy-start.5
  33.5 32.1 %all-to-all-start = ((bf16[128,32,128]{2,1,0:T(8,128)(2,1)}), bf16[128,32,128]{2,1,0:T(8,128)(2,1)S(1)}, u32[]{:S(2)}, u32[]{:S(2)}) async-start(bf16[128,32,128]{2,1,0:T(8,128)(2,1)} %copy.28), calls=%async_computation | async-start | bytes 2097152 | tf_op jit(solution)/shard_map/all_to_all | solution.py:84
  74.8 3.4 %copy-start.1 = (bf16[16,32,8,2,64]{4,3,2,1,0:T(2,128)(2,1)S(1)}, bf16[16,32,8,2,64]{4,3,2,1,0:T(2,128)(2,1)}, u32[]{:S(2)}) copy-start(bf16[16,32,8,2,64]{4,3,2,1,0:T(2,128)(2,1)} %copy.29) | copy-start | bytes 3145732
  79.7 1.6 %copy-start.3 = (bf16[512,8,2,64]{0,3,2,1:T(8,128)(2,1)S(1)}, bf16[512,8,2,64]{0,3,2,1:T(8,128)(2,1)}, u32[]{:S(2)}) copy-start(bf16[512,8,2,64]{0,3,2,1:T(8,128)(2,1)} %copy.31) | copy-start | bytes 3145732
  99.9 23.6 %all-to-all-start.1 = ((bf16[128,32,128]{2,1,0:T(8,128)(2,1)}), bf16[128,32,128]{2,1,0:T(8,128)(2,1)S(1)}, u32[]{:S(2)}, u32[]{:S(2)}) async-start(bf16[128,32,128]{2,1,0:T(8,128)(2,1)} %reshape.223), calls=%async_computation.1 | async-start | bytes 2097152 | tf_op jit(solution)/shard_map/all_to_all | solution.py:100

commit v2 on v1

v2 whole, which is shorter than its diff:
```python
import jax
import jax.numpy as jnp
import numpy as np
from jax import lax
from jax.experimental import pallas as pl
from jax.experimental.pallas import tpu as pltpu
from jax.sharding import PartitionSpec as P

SEG_LEN = 256
BINS = 128
HALF_WIN = 64
SMOOTH = 4
LANES = 128
ALL = ("chan", "tm")
F32 = jnp.float32
BF16 = jnp.bfloat16
VMEM = pl.BlockSpec(memory_space=pltpu.VMEM)


def split(table):
    high = table.astype(BF16)
    low = (table - high.astype(np.float32)).astype(BF16)
    return high, low


def front_tables():
    t_in = np.arange(SEG_LEN)[:, None]
    t_out = np.arange(SEG_LEN)[None, :]
    box_mid = (np.abs(t_in - t_out) <= HALF_WIN).astype(BF16)
    edge = np.arange(LANES)[:, None]
    edge = np.where(edge < HALF_WIN, SEG_LEN + edge, edge - LANES)
    box_edge = (np.abs(edge - t_out) <= HALF_WIN).astype(BF16)
    phase = 2.0 * np.pi / SEG_LEN * (t_in * np.arange(BINS)[None, :] % SEG_LEN)
    forward = np.concatenate([np.cos(phase), -np.sin(phase)], axis=1).astype(np.float32)
    bins = np.arange(BINS)
    band = (np.abs(bins[:, None] - bins[None, :]) <= SMOOTH).astype(BF16)
    band = np.concatenate([band, np.ones((BINS, BINS), BF16)], axis=1)
    return (box_mid, box_edge, *split(forward), band)


def inverse_tables():
    freq = np.arange(BINS)[:, None]
    lag = np.arange(SEG_LEN)[None, :] - BINS
    phase = 2.0 * np.pi / SEG_LEN * (freq * lag % SEG_LEN)
    table = np.stack([np.cos(phase), -np.sin(phase)], axis=1) * (freq > 0)[:, None, :]
    return table.astype(np.float32)


def mxu(a, b):
    return jnp.dot(a, b, preferred_element_type=F32)


def halves(x):
    high = x.astype(BF16)
    return high, (x - high.astype(F32)).astype(BF16)


def front_kernel(
    x_ref, before_ref, after_ref, live_ref, valid_ref,
    mid_ref, edge_ref, high_ref, low_ref, band_ref,
    out_ref, re_ref, im_ref, turned_ref,
):
    rows, span = x_ref.shape
    segs = span // SEG_LEN
    group = 8
    lane = lax.broadcasted_iota(jnp.int32, (rows, LANES), 1)
    first = lax.broadcasted_iota(jnp.int32, (group * rows, BINS), 1) == 0
    for g in range(segs // group):
        own, rim = [], []
        for s in range(g * group, (g + 1) * group):
            start = s * SEG_LEN
            stop = start + SEG_LEN
            own.append(x_ref[:, start:stop])
            left = x_ref[:, start - LANES : start] if s > 0 else before_ref[...]
            right = x_ref[:, stop : stop + LANES] if s < segs - 1 else after_ref[...]
            rim.append(jnp.where(lane < HALF_WIN, right, left))
        x = jnp.concatenate(own, axis=0)
        a_high, a_low = halves(jnp.abs(x))
        e_high, e_low = halves(jnp.abs(jnp.concatenate(rim, axis=0)))
        mid, edge = mid_ref[...], edge_ref[...]
        total = mxu(a_high, mid) + mxu(a_low, mid) + mxu(e_high, edge) + mxu(e_low, edge)
        n_high, n_low = halves(x / (total * (1.0 / (2 * HALF_WIN + 1)) + 1e-05))
        table = high_ref[...]
        spec = mxu(n_high, table) + mxu(n_low, table) + mxu(n_high, low_ref[...])
        re, im = spec[:, :BINS], spec[:, BINS:]
        p_high, p_low = halves(re * re + im * im)
        sums = mxu(p_high, band_ref[...]) + mxu(p_low, band_ref[...])
        floor = sums[:, :BINS] * (1.0 / (2 * SMOOTH + 1)) + sums[:, BINS:] * (0.1 / BINS)
        scale = lax.rsqrt(floor + 1e-06)
        at = pl.ds(g * group * rows, group * rows)
        re_ref[at, :] = jnp.where(first, 1.0, re * scale)
        im_ref[at, :] = jnp.where(first, 0.0, im * scale)
    for c in range(rows):
        picked = pl.ds(c, segs, stride=rows)
        both = jnp.concatenate([re_ref[picked, :], im_ref[picked, :]], axis=0)
        turned_ref[pl.ds(c, BINS, stride=rows), :] = both.T
    mask = (live_ref[...] * valid_ref[...]).astype(F32)
    mask = jnp.concatenate([mask, mask], axis=1)
    whitened = turned_ref[...].reshape(BINS, rows, LANES) * mask[None]
    out_ref[...] = whitened.astype(BF16)


def front(traces, before, after, live, valid):
    rows, span = traces.shape
    segs = span // SEG_LEN
    return pl.pallas_call(
        front_kernel,
        out_shape=jax.ShapeDtypeStruct((BINS, rows, 2 * segs), BF16),
        in_specs=[VMEM] * 10,
        out_specs=VMEM,
        scratch_shapes=[
            pltpu.VMEM((segs * rows, BINS), F32),
            pltpu.VMEM((segs * rows, BINS), F32),
            pltpu.VMEM((BINS * rows, LANES), F32),
        ],
        compiler_params=pltpu.CompilerParams(vmem_limit_bytes=32 << 20),
        name="front",
    )(traces, before, after, live[:, None], valid, *front_tables())


def cross_kernel(got_ref, out_ref, x_ref, r_ref):
    chans, slabs, rows, _ = got_ref.shape
    cols = chans * rows // slabs
    half = LANES // 2
    lane = lax.broadcasted_iota(jnp.int32, (chans * rows, LANES), 1)
    sign = jnp.where(lane < half, 1.0, -1.0)
    for t in range(slabs):
        tile = got_ref[:, t].reshape(chans * rows, LANES)
        turned = (pltpu.roll(tile.astype(F32), half, 1) * sign).astype(BF16)
        at = slice(t * LANES, (t + 1) * LANES)
        x_ref[:, at] = tile
        for u in range(slabs):
            r_ref[2 * u * cols : (2 * u + 1) * cols, at] = tile[u * cols : (u + 1) * cols]
            r_ref[(2 * u + 1) * cols : (2 * u + 2) * cols, at] = turned[u * cols : (u + 1) * cols]
    holds_count = lax.axis_index("chan") * lax.axis_size("tm") + lax.axis_index("tm") == 0
    x = x_ref[...]
    for u in range(0, slabs, 2):
        r = r_ref[2 * u * cols : (2 * u + 4) * cols, :]
        cross = lax.dot_general(x, r, (((1,), (1,)), ((), ())), preferred_element_type=F32)
        for v in range(2):
            part = cross[:, v * LANES : (v + 1) * LANES]
            high = part.astype(BF16)
            out_ref[:, u + v] = high.reshape(chans, rows, LANES)

            @pl.when(holds_count)
            def _():
                whole = high.astype(F32)
                both = whole + pltpu.roll(part - whole, half, 1)
                out_ref[:, u + v] = both.astype(BF16).reshape(chans, rows, LANES)


def cross_spectra(got):
    chans, slabs, rows, lanes = got.shape
    return pl.pallas_call(
        cross_kernel,
        out_shape=jax.ShapeDtypeStruct(got.shape, BF16),
        in_specs=[VMEM],
        out_specs=VMEM,
        scratch_shapes=[
            pltpu.VMEM((chans * rows, slabs * lanes), BF16),
            pltpu.VMEM((2 * chans * rows, slabs * lanes), BF16),
        ],
        compiler_params=pltpu.CompilerParams(vmem_limit_bytes=32 << 20),
        name="cross_spectra",
    )(got)


def body(traces, live_channel, valid_segment):
    span = traces.shape[1]
    chans, slabs = lax.axis_size("chan"), lax.axis_size("tm")
    up = [(i, i + 1) for i in range(slabs - 1)]
    down = [(j, i) for i, j in up]
    before = lax.ppermute(traces[:, span - LANES :], "tm", up)
    after = lax.ppermute(traces[:, :LANES], "tm", down)
    sent = front(traces, before, after, live_channel, valid_segment)
    got = lax.all_to_all(sent, ALL, 0, 0, tiled=True)
    pieces = cross_spectra(got.reshape(chans, slabs, *got.shape[1:]))
    back = lax.all_to_all(pieces.reshape(got.shape), ALL, 0, 0, tiled=True)
    rows, cols = back.shape[1], back.shape[2] // 2
    back = back.reshape(BINS, rows, 2, cols).astype(F32)
    count = back[0, :, 0] + back[0, :, 1]
    lagged = jnp.einsum(
        "fikj,fkl->ijl",
        back,
        jnp.asarray(inverse_tables()),
        precision=lax.Precision.HIGHEST,
        preferred_element_type=F32,
    )
    return lagged * (2.0 / jnp.maximum(count, 1.0))[:, :, None]


def solution(mesh):
    return jax.shard_map(
        body,
        mesh=mesh,
        in_specs=(P("chan", "tm"), P("chan"), P("chan", "tm")),
        out_specs=P("chan", "tm", None),
        check_vma=False,
    )
```

time: 128 us -> 86.5 us (0.68)
  blocking collectives: 0 us -> 57.4 us
  waiting for transfers between devices: 37.8 us -> 0.11 us
  local copies, waits for them, and re-layouts: 41.2 us -> 9.47 us
  starting transfers between devices: 23.3 us -> 5.94 us
  other arithmetic: 13.6 us -> 0.6 us
  Pallas kernels: 0 us -> 10.1 us
  matrix products: 11.5 us -> 2.33 us
    all_to_all x0 -> x2, blocking collectives: none -> 57.4 us  [the longest x1 33.3 us: body(): got = lax.all_to_all(sent, ALL, 0, 0, tiled=True)]
    all_to_all x2 -> x0, waiting for transfers between devices: 37.2 us -> none  [the longest x1 18.8 us: body(): got = lax.all_to_all(sent, ALL, 0, 0, tiled=True)]
    all_to_all x2 -> x0, starting transfers between devices: 18 us -> none  [the longest x1 13.3 us: body(): got = lax.all_to_all(sent, ALL, 0, 0, tiled=True)]
    another operation x6 -> x0, local copies, waits for them, and re-layouts: 11.8 us -> none  [the longest x4 6.86 us: body(): pieces = jnp.stack([rounded, cross_imag], axis=0).astype(jnp.bfloat16)]
    pallas_call x0 -> x2, Pallas kernels: none -> 10.1 us  [the longest x1 7 us: front(): pl.pallas_call(front_kernel, out_shape=jax.ShapeDtypeStruct((BINS, rows,...]
    reshape x4 -> x0, local copies, waits for them, and re-layouts: 9.33 us -> none  [the longest x1 4.75 us: body(): jnp.transpose(pieces, (1, 3, 2, 0, 4)).reshape(BINS, chan_rows, 2 * cols)]
    dot_general x6 -> x1, matrix products: 11.5 us -> 2.33 us  [body(): jnp.einsum('fikj,fkl->ijl', back, jnp.asarray(inverse_tables()), precisio...]
    transpose x1 -> x0, other arithmetic: 6.36 us -> none  [body(): jnp.transpose(pieces, (1, 3, 2, 0, 4)).reshape(BINS, chan_rows, 2 * cols)]
  transfers between devices with their start and end apart: 4 -> 2, of which waited for: 3 -> 1; matrix products, arithmetic and copies ran while one was open for 2% -> 1% of each run, Pallas kernels for 0% -> 0%
where the time goes in v2:
time: 86.5 us; the launch traced here: 86 us
  blocking collectives  57.4 us (66%)
  Pallas kernels  10.1 us (12%)
  local copies, waits for them, and re-layouts  9.47 us (11%)
  starting transfers between devices  5.94 us (7%)
  matrix products  2.33 us (3%)
    all_to_all x1, blocking collectives, body(): got = lax.all_to_all(sent, ALL, 0, 0, tiled=True)  33.3 us
    all_to_all x1, blocking collectives, body(): back = lax.all_to_all(pieces.reshape(got.shape), ALL, 0, 0, tiled=True)  24.1 us
    unnamed x16, local copies, waits for them, and re-layouts  7.03 us
    pallas_call x1, Pallas kernels, front(): pl.pallas_call(front_kernel, out_shape=jax.ShapeDtypeStruct((BINS, rows,...  7 us
    ppermute x1, starting transfers between devices, body(): before = lax.ppermute(traces[:, span - LANES:], 'tm', up)  4.66 us
    pallas_call x1, Pallas kernels, cross_spectra(): pl.pallas_call(cross_kernel, out_shape=jax.ShapeDtypeStruct(got.shape, BF...  3.09 us
    dot_general x1, matrix products, body(): jnp.einsum('fikj,fkl->ijl', back, jnp.asarray(inverse_tables()), precisio...  2.33 us
  transfers between devices with their start and end apart: 2, of which 1 were waited for; matrix products, arithmetic and copies ran while one was open for 1% of the time, Pallas kernels for 0%

profile of v2, /device:TPU:1, one launch (start us, length us, event | category | flops | bytes accessed | tf_op | source)
XLA Modules:
  0.0 86.0 jit_solution(12390086297169976508)
XLA Ops:
  0.0 0.7 fusion.3
  0.7 1.3 %collective-permute-start.1 = (f32[32,128]{1,0:T(8,128)S(1)}, f32[32,128]{1,0:T(8,128)S(1)}, u32[]{:S(2)}, u32[]{:S(2)}) collective-permute-start(f32[32,128]{1,0:T(8,128)S(1)} %get-tuple-element.5), channel_id=1, source_target_pairs={{1,0},{2,1},{3,2},{4,3},{5,4},{6,5},{7,6},{9,8},{10,9},{11,10},{12... | collective-permute-start | bytes 49160 | tf_op jit(solution)/shard_map/ppermute | solution.py:174
  2.0 4.7 %collective-permute-start = (f32[32,128]{1,0:T(8,128)S(1)}, f32[32,128]{1,0:T(8,128)S(1)}, u32[]{:S(2)}, u32[]{:S(2)}) collective-permute-start(f32[32,128]{1,0:T(8,128)S(1)} %get-tuple-element.6), channel_id=1, source_target_pairs={{0,1},{1,2},{2,3},{3,4},{4,5},{5,6},{6,7},{8,9},{9,10},{10,11},{11... | collective-permute-start | bytes 49160 | tf_op jit(solution)/shard_map/ppermute | solution.py:173
  6.7 0.7 copy.12.live_ref
  7.4 0.0 collective-permute-done.1.after_ref
  7.4 0.1 collective-permute-done.before_ref
  7.5 0.0 copy-start
  7.5 1.6 %copy-done = f32[32,16384]{1,0:T(8,128)S(1)} copy-done((f32[32,16384]{1,0:T(8,128)S(1)}, f32[32,16384]{1,0:T(8,128)}, u32[]{:S(2)}) %copy-start) | copy-done | bytes 2097176
  9.1 0.9 %copy-done.1 = bf16[256,256]{1,0:T(8,128)(2,1)S(1)} copy-done((bf16[256,256]{1,0:T(8,128)(2,1)S(1)}, bf16[256,256]{1,0:T(8,128)(2,1)}, u32[]{:S(2)}) %copy-start.1) | copy-done | bytes 131096
  10.0 0.9 %copy-done.2 = bf16[256,256]{1,0:T(8,128)(2,1)S(1)} copy-done((bf16[256,256]{1,0:T(8,128)(2,1)S(1)}, bf16[256,256]{1,0:T(8,128)(2,1)}, u32[]{:S(2)}) %copy-start.2) | copy-done | bytes 131096
  10.9 0.9 %copy-done.3 = bf16[256,256]{1,0:T(8,128)(2,1)S(1)} copy-done((bf16[256,256]{1,0:T(8,128)(2,1)S(1)}, bf16[256,256]{1,0:T(8,128)(2,1)}, u32[]{:S(2)}) %copy-start.3) | copy-done | bytes 131096
  11.9 0.8 copy-done.4
  12.7 0.8 copy-done.5
  13.5 0.7 copy-done.6
  14.2 7.0 %front.1 = bf16[128,32,128]{2,1,0:T(8,128)(2,1)S(1)} custom-call(f32[32,16384]{1,0:T(8,128)S(1)} %copy-done, f32[32,128]{1,0:T(8,128)S(1)} %collective-permute-done.before_ref, f32[32,128]{1,0:T(8,128)S(1)} %collective-permute-done.1.after_ref, s32[32,1]{1,0:T(8,128)S(1)} %copy.12.live_ref, s32[32,64]{1,0:T(8,128)S(1)} %copy-done.6, ...), custom_call_target="tpu_custom_call" | custom-call | tf_op jit(solution)/shard_map/front/pallas_call | solution.py:106
  21.3 33.3 %all_to_all.10 = bf16[128,32,128]{2,1,0:T(8,128)(2,1)S(1)} all-to-all(bf16[128,32,128]{2,1,0:T(8,128)(2,1)S(1)} %front.1), channel_id=1, replica_groups=mesh['chan'=16,'tm'=8] {'chan','tm'}, dimensions={0} | all-to-all | bytes 2097152 | tf_op jit(solution)/shard_map/all_to_all | solution.py:176
  54.6 3.1 %cross_spectra.1 = bf16[16,8,32,128]{3,2,1,0:T(8,128)(2,1)S(1)} custom-call(bf16[16,8,32,128]{3,2,1,0:T(8,128)(2,1)S(1)} %bitcast.11), custom_call_target="tpu_custom_call" | custom-call | tf_op jit(solution)/shard_map/cross_spectra/pallas_call | solution.py:154
  57.7 24.1 %all_to_all.11 = bf16[128,32,128]{2,1,0:T(8,128)(2,1)S(1)} all-to-all(bf16[128,32,128]{2,1,0:T(8,128)(2,1)S(1)} %bitcast.12), channel_id=1, replica_groups=mesh['chan'=16,'tm'=8] {'chan','tm'}, dimensions={0} | all-to-all | bytes 2097152 | tf_op jit(solution)/shard_map/all_to_all | solution.py:178
  81.7 1.0 %copy.13 = bf16[128,32,128]{0,2,1:T(8,128)(2,1)S(1)} copy(bf16[128,32,128]{2,1,0:T(8,128)(2,1)S(1)} %all_to_all.11) | data formatting | bytes 2097152 | tf_op jit(solution)/shard_map/all_to_all | solution.py:178
  82.7 0.0 copy-start.7
  82.7 0.2 bitcast_convert_fusion
  83.0 0.4 fusion.2
  83.3 0.3 copy-done.7
  83.7 2.3 %bitcast_multiply_fusion = f32[32,64,256]{2,1,0:T(8,128)} fusion(bf16[128,32,2,64]{0,3,2,1:T(8,128)(2,1)S(1)} %bitcast.13, f32[128,2,256,1]{2,0,1,3:T(8,128)S(1)} %copy-done.7, f32[32,64]{1,0:T(8,128)S(1)} %fusion.2), kind=kOutput, calls=%fused_computation | convolution fusion | flops 1611137024 | bytes 3416064 | tf_op jit(solution)/shard_map/fikj,fkl->ijl/dot_general | solution.py:182
  (6 shorter events, 0.0 us)
Async XLA Ops:
  0.7 6.7 %collective-permute-start.1 = (f32[32,128]{1,0:T(8,128)S(1)}, f32[32,128]{1,0:T(8,128)S(1)}, u32[]{:S(2)}, u32[]{:S(2)}) collective-permute-start(f32[32,128]{1,0:T(8,128)S(1)} %get-tuple-element.5), channel_id=1, source_target_pairs={{1,0},{2,1},{3,2},{4,3},{5,4},{6,5},{7,6},{9,8},{10,9},{11,10},{12... | collective-permute-start | bytes 49160 | tf_op jit(solution)/shard_map/ppermute | solution.py:174
  2.0 5.5 %collective-permute-start = (f32[32,128]{1,0:T(8,128)S(1)}, f32[32,128]{1,0:T(8,128)S(1)}, u32[]{:S(2)}, u32[]{:S(2)}) collective-permute-start(f32[32,128]{1,0:T(8,128)S(1)} %get-tuple-element.6), channel_id=1, source_target_pairs={{0,1},{1,2},{2,3},{3,4},{4,5},{5,6},{6,7},{8,9},{9,10},{10,11},{11... | collective-permute-start | bytes 49160 | tf_op jit(solution)/shard_map/ppermute | solution.py:173
  7.5 1.6 %copy-start = (f32[32,16384]{1,0:T(8,128)S(1)}, f32[32,16384]{1,0:T(8,128)}, u32[]{:S(2)}) copy-start(f32[32,16384]{1,0:T(8,128)} %x_ref.1) | copy-start | bytes 6291460
  9.1 0.9 %copy-start.1 = (bf16[256,256]{1,0:T(8,128)(2,1)S(1)}, bf16[256,256]{1,0:T(8,128)(2,1)}, u32[]{:S(2)}) copy-start(bf16[256,256]{1,0:T(8,128)(2,1)} %constant.19.clone.low_ref) | copy-start | bytes 393220
  10.0 0.9 %copy-start.2 = (bf16[256,256]{1,0:T(8,128)(2,1)S(1)}, bf16[256,256]{1,0:T(8,128)(2,1)}, u32[]{:S(2)}) copy-start(bf16[256,256]{1,0:T(8,128)(2,1)} %constant.18.clone.high_ref) | copy-start | bytes 393220
  10.9 0.9 %copy-start.3 = (bf16[256,256]{1,0:T(8,128)(2,1)S(1)}, bf16[256,256]{1,0:T(8,128)(2,1)}, u32[]{:S(2)}) copy-start(bf16[256,256]{1,0:T(8,128)(2,1)} %constant.16.clone.mid_ref) | copy-start | bytes 393220
  11.9 0.8 copy-start.4
  12.7 0.8 copy-start.5
  13.5 0.7 copy-start.6
  82.7 1.0 %copy-start.7 = (f32[128,2,256,1]{2,0,1,3:T(8,128)S(1)}, f32[128,2,256,1]{2,0,1,3:T(8,128)}, u32[]{:S(2)}) copy-start(f32[128,2,256,1]{2,0,1,3:T(8,128)} %constant.22) | copy-start | bytes 786436

commit v3 on v2

--- a/solution.py
+++ b/solution.py
@@ -35,7 +35,7 @@
     bins = np.arange(BINS)
     band = (np.abs(bins[:, None] - bins[None, :]) <= SMOOTH).astype(BF16)
     band = np.concatenate([band, np.ones((BINS, BINS), BF16)], axis=1)
-    return (box_mid, box_edge, *split(forward), band)
+    return np.stack([box_mid, np.tile(box_edge, (2, 1)), *split(forward), np.tile(band, (2, 1))])
 
 
 def inverse_tables():
@@ -55,67 +55,140 @@
     return high, (x - high.astype(F32)).astype(BF16)
 
 
-def front_kernel(
-    x_ref, before_ref, after_ref, live_ref, valid_ref,
-    mid_ref, edge_ref, high_ref, low_ref, band_ref,
-    out_ref, re_ref, im_ref, turned_ref,
-):
+def whiten(x, rim, table_ref):
+    mid, edge, high, low, band = (table_ref[i] for i in range(5))
+    a_high, a_low = halves(jnp.abs(x))
+    e_both = jnp.concatenate(halves(jnp.abs(rim)), axis=1)
+    total = mxu(a_high, mid) + mxu(a_low, mid) + mxu(e_both, edge)
+    n_high, n_low = halves(x / (total * (1.0 / (2 * HALF_WIN + 1)) + 1e-05))
+    spec = mxu(n_high, high) + mxu(n_low, high) + mxu(n_high, low)
+    re, im = spec[:, :BINS], spec[:, BINS:]
+    sums = mxu(jnp.concatenate(halves(re * re + im * im), axis=1), band)
+    floor = sums[:, :BINS] * (1.0 / (2 * SMOOTH + 1)) + sums[:, BINS:] * (0.1 / BINS)
+    scale = lax.rsqrt(floor + 1e-06)
+    first = lax.broadcasted_iota(jnp.int32, re.shape, 1) == 0
+    return jnp.where(first, 1.0, re * scale), jnp.where(first, 0.0, im * scale)
+
+
+def beside(right, left):
+    lane = lax.broadcasted_iota(jnp.int32, right.shape, 1)
+    return jnp.where(lane < HALF_WIN, right, left)
+
+
+GROUP = 8
+END = SEG_LEN + LANES
+
+
+def spectra_kernel(x_hbm, table_hbm, re_ref, im_ref, ends_ref, x_ref, table_ref, sems):
     rows, span = x_ref.shape
     segs = span // SEG_LEN
-    group = 8
-    lane = lax.broadcasted_iota(jnp.int32, (rows, LANES), 1)
-    first = lax.broadcasted_iota(jnp.int32, (group * rows, BINS), 1) == 0
-    for g in range(segs // group):
+    width = GROUP * SEG_LEN
+    groups = span // width
+    copies = [
+        pltpu.make_async_copy(
+            x_hbm.at[:, g * width : (g + 1) * width],
+            x_ref.at[:, g * width : (g + 1) * width],
+            sems.at[g],
+        )
+        for g in range(groups)
+    ]
+    table_copy = pltpu.make_async_copy(table_hbm, table_ref, sems.at[groups])
+    copies[0].start()
+    table_copy.start()
+    for copy in copies[1:]:
+        copy.start()
+    copies[0].wait()
+    table_copy.wait()
+    nothing = jnp.zeros((rows, LANES), F32)
+    for g in range(groups):
+        if g + 1 < groups:
+            copies[g + 1].wait()
         own, rim = [], []
-        for s in range(g * group, (g + 1) * group):
+        for s in range(g * GROUP, (g + 1) * GROUP):
             start = s * SEG_LEN
             stop = start + SEG_LEN
             own.append(x_ref[:, start:stop])
-            left = x_ref[:, start - LANES : start] if s > 0 else before_ref[...]
-            right = x_ref[:, stop : stop + LANES] if s < segs - 1 else after_ref[...]
-            rim.append(jnp.where(lane < HALF_WIN, right, left))
-        x = jnp.concatenate(own, axis=0)
-        a_high, a_low = halves(jnp.abs(x))
-        e_high, e_low = halves(jnp.abs(jnp.concatenate(rim, axis=0)))
-        mid, edge = mid_ref[...], edge_ref[...]
-        total = mxu(a_high, mid) + mxu(a_low, mid) + mxu(e_high, edge) + mxu(e_low, edge)
-        n_high, n_low = halves(x / (total * (1.0 / (2 * HALF_WIN + 1)) + 1e-05))
-        table = high_ref[...]
-        spec = mxu(n_high, table) + mxu(n_low, table) + mxu(n_high, low_ref[...])
-        re, im = spec[:, :BINS], spec[:, BINS:]
-        p_high, p_low = halves(re * re + im * im)
-        sums = mxu(p_high, band_ref[...]) + mxu(p_low, band_ref[...])
-        floor = sums[:, :BINS] * (1.0 / (2 * SMOOTH + 1)) + sums[:, BINS:] * (0.1 / BINS)
-        scale = lax.rsqrt(floor + 1e-06)
-        at = pl.ds(g * group * rows, group * rows)
-        re_ref[at, :] = jnp.where(first, 1.0, re * scale)
-        im_ref[at, :] = jnp.where(first, 0.0, im * scale)
+            left = x_ref[:, start - LANES : start] if s > 0 else nothing
+            right = x_ref[:, stop : stop + LANES] if s < segs - 1 else nothing
+            rim.append(beside(right, left))
+        re, im = whiten(jnp.concatenate(own, axis=0), jnp.concatenate(rim, axis=0), table_ref)
+        at = slice(g * GROUP * rows, (g + 1) * GROUP * rows)
+        re_ref[at, :] = re
+        im_ref[at, :] = im
+    ends_ref[:, :END] = x_ref[:, :END]
+    ends_ref[:, END:] = x_ref[:, span - END :]
+
+
+def spectra(traces, table):
+    rows, span = traces.shape
+    segs = span // SEG_LEN
+    half = jax.ShapeDtypeStruct((segs * rows, BINS), F32)
+    return pl.pallas_call(
+        spectra_kernel,
+        out_shape=(half, half, jax.ShapeDtypeStruct((rows, 2 * END), F32)),
+        in_specs=[pl.BlockSpec(memory_space=pltpu.HBM)] * 2,
+        out_specs=(VMEM, VMEM, VMEM),
+        scratch_shapes=[
+            pltpu.VMEM(traces.shape, F32),
+            pltpu.VMEM(table.shape, BF16),
+            pltpu.SemaphoreType.DMA((span // (GROUP * SEG_LEN) + 1,)),
+        ],
+        compiler_params=pltpu.CompilerParams(vmem_limit_bytes=32 << 20),
+        name="spectra",
+    )(
+        pltpu.with_memory_space_constraint(traces, pltpu.HBM),
+        pltpu.with_memory_space_constraint(table, pltpu.HBM),
+    )
+
+
+def turn_kernel(
+    re_ref, im_ref, ends_ref, before_ref, after_ref, live_ref, valid_ref, table_ref,
+    out_ref, turned_ref,
+):
+    rows = ends_ref.shape[0]
+    segs = re_ref.shape[0] // rows
+    x = jnp.concatenate([ends_ref[:, :SEG_LEN], ends_ref[:, END + LANES :]], axis=0)
+    rim = [
+        beside(ends_ref[:, SEG_LEN:END], before_ref[...]),
+        beside(after_ref[...], ends_ref[:, END : END + LANES]),
+    ]
+    fixed = whiten(x, jnp.concatenate(rim, axis=0), table_ref)
+    row = lax.broadcasted_iota(jnp.int32, (8, BINS), 0)
     for c in range(rows):
-        picked = pl.ds(c, segs, stride=rows)
-        both = jnp.concatenate([re_ref[picked, :], im_ref[picked, :]], axis=0)
-        turned_ref[pl.ds(c, BINS, stride=rows), :] = both.T
-    mask = (live_ref[...] * valid_ref[...]).astype(F32)
+        pieces = []
+        for ref, ends in zip((re_ref, im_ref), fixed):
+            picked = ref[pl.ds(c, segs, stride=rows), :]
+            pieces += [
+                jnp.where(row == 0, ends[c : c + 1], picked[:8]),
+                picked[8 : segs - 8],
+                jnp.where(row == 7, ends[rows + c : rows + c + 1], picked[segs - 8 :]),
+            ]
+        turned_ref[pl.ds(c, BINS, stride=rows), :] = jnp.concatenate(pieces, axis=0).T
+    live = jnp.broadcast_to(live_ref[...].astype(F32), (rows, rows))
+    here = [lax.broadcasted_iota(jnp.int32, (rows, rows), axis) for axis in range(2)]
+    live = jnp.sum(jnp.where(here[0] == here[1], live, 0.0), axis=1, keepdims=True)
+    mask = live * valid_ref[...].astype(F32)
     mask = jnp.concatenate([mask, mask], axis=1)
     whitened = turned_ref[...].reshape(BINS, rows, LANES) * mask[None]
     out_ref[...] = whitened.astype(BF16)
 
 
+def turn(parts, before, after, live, valid, table):
+    rows, segs = valid.shape
+    return pl.pallas_call(
+        turn_kernel,
+        out_shape=jax.ShapeDtypeStruct((BINS, rows, 2 * segs), BF16),
+        in_specs=[VMEM] * 8,
+        out_specs=VMEM,
+        scratch_shapes=[pltpu.VMEM((BINS * rows, LANES), F32)],
+        compiler_params=pltpu.CompilerParams(vmem_limit_bytes=32 << 20),
+        name="turn",
+    )(*parts, before, after, live[None, :], valid, table)
+
+
 def front(traces, before, after, live, valid):
-    rows, span = traces.shape
-    segs = span // SEG_LEN
-    return pl.pallas_call(
-        front_kernel,
-        out_shape=jax.ShapeDtypeStruct((BINS, rows, 2 * segs), BF16),
-        in_specs=[VMEM] * 10,
-        out_specs=VMEM,
-        scratch_shapes=[
-            pltpu.VMEM((segs * rows, BINS), F32),
-            pltpu.VMEM((segs * rows, BINS), F32),
-            pltpu.VMEM((BINS * rows, LANES), F32),
-        ],
-        compiler_params=pltpu.CompilerParams(vmem_limit_bytes=32 << 20),
-        name="front",
-    )(traces, before, after, live[:, None], valid, *front_tables())
+    table = jnp.asarray(front_tables())
+    return turn(spectra(traces, table), before, after, live, valid, table)
 
 
 def cross_kernel(got_ref, out_ref, x_ref, r_ref):
@@ -132,21 +205,25 @@
         for u in range(slabs):
             r_ref[2 * u * cols : (2 * u + 1) * cols, at] = tile[u * cols : (u + 1) * cols]
             r_ref[(2 * u + 1) * cols : (2 * u + 2) * cols, at] = turned[u * cols : (u + 1) * cols]
-    holds_count = lax.axis_index("chan") * lax.axis_size("tm") + lax.axis_index("tm") == 0
+    middle = slabs // 2 * LANES
+
+    @pl.when(lax.axis_index("chan") * lax.axis_size("tm") + lax.axis_index("tm") == 0)
+    def _():
+        for u in range(slabs):
+            real = slice(2 * u * cols, (2 * u + 1) * cols)
+            imag = slice((2 * u + 1) * cols, (2 * u + 2) * cols)
+            own = slice(u * cols, (u + 1) * cols)
+            r_ref[real, middle:] = jnp.zeros((cols, slabs * LANES - middle), BF16)
+            r_ref[imag, :middle] = jnp.zeros((cols, middle), BF16)
+            r_ref[imag, middle:] = x_ref[own, middle:]
+
     x = x_ref[...]
     for u in range(0, slabs, 2):
         r = r_ref[2 * u * cols : (2 * u + 4) * cols, :]
         cross = lax.dot_general(x, r, (((1,), (1,)), ((), ())), preferred_element_type=F32)
         for v in range(2):
             part = cross[:, v * LANES : (v + 1) * LANES]
-            high = part.astype(BF16)
-            out_ref[:, u + v] = high.reshape(chans, rows, LANES)
-
-            @pl.when(holds_count)
-            def _():
-                whole = high.astype(F32)
-                both = whole + pltpu.roll(part - whole, half, 1)
-                out_ref[:, u + v] = both.astype(BF16).reshape(chans, rows, LANES)
+            out_ref[:, u + v] = part.astype(BF16).reshape(chans, rows, LANES)
 
 
 def cross_spectra(got):

time: 86.5 us -> 78.8 us (0.911)
  local copies, waits for them, and re-layouts: 9.47 us -> 2.12 us
  Pallas kernels: 10.1 us -> 12.3 us
  blocking collectives: 57.4 us -> 55.2 us
    unnamed x16 -> x8, local copies, waits for them, and re-layouts: 7.03 us -> 0.34 us
    pallas_call x1 -> x2, Pallas kernels: 7 us -> 10.2 us  [the longest x1 7.08 us: spectra(): pl.pallas_call(spectra_kernel, out_shape=(half, half, jax.ShapeDtypeStruc...]
    all_to_all x1, blocking collectives: 33.3 us -> 31.9 us  [body(): got = lax.all_to_all(sent, ALL, 0, 0, tiled=True)]
    pallas_call x1, Pallas kernels: 3.09 us -> 2.05 us  [cross_spectra(): pl.pallas_call(cross_kernel, out_shape=jax.ShapeDtypeStruct(got.shape, BF...]
  transfers between devices with their start and end apart: 2 -> 2, of which waited for: 1 -> 0; matrix products, arithmetic and copies ran while one was open for 1% -> 0% of each run, Pallas kernels for 0% -> 9%
where the time goes in v3:
time: 78.8 us; the launch traced here: 78.5 us
  blocking collectives  55.2 us (70%)
  Pallas kernels  12.3 us (16%)
  starting transfers between devices  5.94 us (8%)
  matrix products  2.33 us (3%)
  local copies, waits for them, and re-layouts  2.12 us (3%)
    all_to_all x1, blocking collectives, body(): got = lax.all_to_all(sent, ALL, 0, 0, tiled=True)  31.9 us
    all_to_all x1, blocking collectives, body(): back = lax.all_to_all(pieces.reshape(got.shape), ALL, 0, 0, tiled=True)  23.2 us
    pallas_call x1, Pallas kernels, spectra(): pl.pallas_call(spectra_kernel, out_shape=(half, half, jax.ShapeDtypeStruc...  7.08 us
    ppermute x1, starting transfers between devices, body(): before = lax.ppermute(traces[:, span - LANES:], 'tm', up)  4.66 us
    pallas_call x1, Pallas kernels, turn(): pl.pallas_call(turn_kernel, out_shape=jax.ShapeDtypeStruct((BINS, rows, 2...  3.14 us
    dot_general x1, matrix products, body(): jnp.einsum('fikj,fkl->ijl', back, jnp.asarray(inverse_tables()), precisio...  2.33 us
    pallas_call x1, Pallas kernels, cross_spectra(): pl.pallas_call(cross_kernel, out_shape=jax.ShapeDtypeStruct(got.shape, BF...  2.05 us
  transfers between devices with their start and end apart: 2, of which 0 were waited for; matrix products, arithmetic and copies ran while one was open for 0% of the time, Pallas kernels for 9%

profile of v3, /device:TPU:1, one launch (start us, length us, event | category | flops | bytes accessed | tf_op | source)
XLA Modules:
  0.0 78.5 jit_solution(11446842111908793393)
XLA Ops:
  0.0 0.0 copy-start
  0.0 0.0 copy-start.1
  0.0 0.0 copy-start.2
  0.0 0.8 %fusion.3 = (f32[32,128]{1,0:T(8,128)S(1)}, f32[32,128]{1,0:T(8,128)S(1)}) fusion(f32[32,16384]{1,0:T(8,128)} %x_hbm.1), kind=kLoop, calls=%fused_computation.6 | loop fusion | bytes 65536 | tf_op jit(solution)/shard_map/slice | solution.py:251
  0.8 1.3 %collective-permute-start.1 = (f32[32,128]{1,0:T(8,128)S(1)}, f32[32,128]{1,0:T(8,128)S(1)}, u32[]{:S(2)}, u32[]{:S(2)}) collective-permute-start(f32[32,128]{1,0:T(8,128)S(1)} %get-tuple-element.11), channel_id=1, source_target_pairs={{1,0},{2,1},{3,2},{4,3},{5,4},{6,5},{7,6},{9,8},{10,9},{11,10},{12... | collective-permute-start | bytes 49160 | tf_op jit(solution)/shard_map/ppermute | solution.py:251
  2.1 4.7 %collective-permute-start = (f32[32,128]{1,0:T(8,128)S(1)}, f32[32,128]{1,0:T(8,128)S(1)}, u32[]{:S(2)}, u32[]{:S(2)}) collective-permute-start(f32[32,128]{1,0:T(8,128)S(1)} %get-tuple-element.12), channel_id=1, source_target_pairs={{0,1},{1,2},{2,3},{3,4},{4,5},{5,6},{6,7},{8,9},{9,10},{10,11},{11... | collective-permute-start | bytes 49160 | tf_op jit(solution)/shard_map/ppermute | solution.py:250
  6.8 7.1 %spectra.1 = (f32[2048,128]{1,0:T(8,128)S(1)}, f32[2048,128]{1,0:T(8,128)S(1)}, f32[32,768]{1,0:T(8,128)S(1)}) custom-call(f32[32,16384]{1,0:T(8,128)} %x_hbm.1, bf16[5,256,256]{2,1,0:T(8,128)(2,1)} %constant.8.clone.table_hbm.table_ref), custom_call_target="tpu_custom_call" | custom-call | tf_op jit(solution)/shard_map/spectra/pallas_call | solution.py:126
  13.9 0.0 collective-permute-done.1.after_ref
  13.9 0.0 collective-permute-done.before_ref
  13.9 0.0 copy-done
  13.9 0.0 copy-done.1
  13.9 0.0 copy-done.2
  13.9 3.1 %turn.1 = bf16[128,32,128]{2,1,0:T(8,128)(2,1)S(1)} custom-call(f32[2048,128]{1,0:T(8,128)S(1)} %get-tuple-element.8.re_ref, f32[2048,128]{1,0:T(8,128)S(1)} %get-tuple-element.9.im_ref, f32[32,768]{1,0:T(8,128)S(1)} %get-tuple-element.10.ends_ref, f32[32,128]{1,0:T(8,128)S(1)} %collective-permute-done.before_ref, ...), custom_call_target="tpu_custom_call" | custom-call | tf_op jit(solution)/shard_map/turn/pallas_call | solution.py:178
  17.1 31.9 %all_to_all.10 = bf16[128,32,128]{2,1,0:T(8,128)(2,1)S(1)} all-to-all(bf16[128,32,128]{2,1,0:T(8,128)(2,1)S(1)} %turn.1), channel_id=1, replica_groups=mesh['chan'=16,'tm'=8] {'chan','tm'}, dimensions={0} | all-to-all | bytes 2097152 | tf_op jit(solution)/shard_map/all_to_all | solution.py:253
  49.0 2.1 %cross_spectra.1 = bf16[16,8,32,128]{3,2,1,0:T(8,128)(2,1)S(1)} custom-call(bf16[16,8,32,128]{3,2,1,0:T(8,128)(2,1)S(1)} %bitcast.11), custom_call_target="tpu_custom_call" | custom-call | tf_op jit(solution)/shard_map/cross_spectra/pallas_call | solution.py:231
  51.0 23.2 %all_to_all.11 = bf16[128,32,128]{2,1,0:T(8,128)(2,1)S(1)} all-to-all(bf16[128,32,128]{2,1,0:T(8,128)(2,1)S(1)} %bitcast.12), channel_id=1, replica_groups=mesh['chan'=16,'tm'=8] {'chan','tm'}, dimensions={0} | all-to-all | bytes 2097152 | tf_op jit(solution)/shard_map/all_to_all | solution.py:255
  74.3 1.0 %copy.7 = bf16[128,32,128]{0,2,1:T(8,128)(2,1)S(1)} copy(bf16[128,32,128]{2,1,0:T(8,128)(2,1)S(1)} %all_to_all.11) | data formatting | bytes 2097152 | tf_op jit(solution)/shard_map/all_to_all | solution.py:255
  75.2 0.0 copy-start.3
  75.3 0.2 bitcast_convert_fusion
  75.5 0.4 fusion.2
  75.9 0.3 copy-done.3
  76.2 2.3 %bitcast_multiply_fusion = f32[32,64,256]{2,1,0:T(8,128)} fusion(bf16[128,32,2,64]{0,3,2,1:T(8,128)(2,1)S(1)} %bitcast.14, f32[128,2,256,1]{2,0,1,3:T(8,128)S(1)} %copy-done.3, f32[32,64]{1,0:T(8,128)S(1)} %fusion.2), kind=kOutput, calls=%fused_computation | convolution fusion | flops 1611137024 | bytes 3416064 | tf_op jit(solution)/shard_map/fikj,fkl->ijl/dot_general | solution.py:259
Async XLA Ops:
  0.0 13.9 %copy-start = (bf16[5,256,256]{2,1,0:T(8,128)(2,1)S(1)}, bf16[5,256,256]{2,1,0:T(8,128)(2,1)}, u32[]{:S(2)}) copy-start(bf16[5,256,256]{2,1,0:T(8,128)(2,1)} %constant.8.clone.table_hbm.table_ref) | copy-start | bytes 1966084
  0.0 13.9 %copy-start.1 = (s32[32,64]{1,0:T(8,128)S(1)}, s32[32,64]{1,0:T(8,128)}, u32[]{:S(2)}) copy-start(s32[32,64]{1,0:T(8,128)} %valid_ref.1) | copy-start | bytes 24580
  0.0 13.9 %copy-start.2 = (s32[32]{0:T(128)S(1)}, s32[32]{0:T(128)}, u32[]{:S(2)}) copy-start(s32[32]{0:T(128)} %param.6) | copy-start | bytes 388
  0.8 13.0 %collective-permute-start.1 = (f32[32,128]{1,0:T(8,128)S(1)}, f32[32,128]{1,0:T(8,128)S(1)}, u32[]{:S(2)}, u32[]{:S(2)}) collective-permute-start(f32[32,128]{1,0:T(8,128)S(1)} %get-tuple-element.11), channel_id=1, source_target_pairs={{1,0},{2,1},{3,2},{4,3},{5,4},{6,5},{7,6},{9,8},{10,9},{11,10},{12... | collective-permute-start | bytes 49160 | tf_op jit(solution)/shard_map/ppermute | solution.py:251
  2.1 11.8 %collective-permute-start = (f32[32,128]{1,0:T(8,128)S(1)}, f32[32,128]{1,0:T(8,128)S(1)}, u32[]{:S(2)}, u32[]{:S(2)}) collective-permute-start(f32[32,128]{1,0:T(8,128)S(1)} %get-tuple-element.12), channel_id=1, source_target_pairs={{0,1},{1,2},{2,3},{3,4},{4,5},{5,6},{6,7},{8,9},{9,10},{10,11},{11... | collective-permute-start | bytes 49160 | tf_op jit(solution)/shard_map/ppermute | solution.py:250
  75.2 1.0 %copy-start.3 = (f32[128,2,256,1]{2,0,1,3:T(8,128)S(1)}, f32[128,2,256,1]{2,0,1,3:T(8,128)}, u32[]{:S(2)}) copy-start(f32[128,2,256,1]{2,0,1,3:T(8,128)} %constant.10) | copy-start | bytes 786436

commit v4 on v3

--- a/solution.py
+++ b/solution.py
@@ -55,15 +55,23 @@
     return high, (x - high.astype(F32)).astype(BF16)
 
 
-def whiten(x, rim, table_ref):
-    mid, edge, high, low, band = (table_ref[i] for i in range(5))
+def level(x, rim, table_ref):
+    mid, edge = table_ref[0], table_ref[1]
     a_high, a_low = halves(jnp.abs(x))
     e_both = jnp.concatenate(halves(jnp.abs(rim)), axis=1)
     total = mxu(a_high, mid) + mxu(a_low, mid) + mxu(e_both, edge)
-    n_high, n_low = halves(x / (total * (1.0 / (2 * HALF_WIN + 1)) + 1e-05))
-    spec = mxu(n_high, high) + mxu(n_low, high) + mxu(n_high, low)
+    return halves(x / (total * (1.0 / (2 * HALF_WIN + 1)) + 1e-05))
+
+
+def transform(high, low, table_ref):
+    table = table_ref[2]
+    spec = mxu(high, table) + mxu(low, table) + mxu(high, table_ref[3])
     re, im = spec[:, :BINS], spec[:, BINS:]
-    sums = mxu(jnp.concatenate(halves(re * re + im * im), axis=1), band)
+    return re, im, jnp.concatenate(halves(re * re + im * im), axis=1)
+
+
+def whiten(re, im, power, table_ref):
+    sums = mxu(power, table_ref[4])
     floor = sums[:, :BINS] * (1.0 / (2 * SMOOTH + 1)) + sums[:, BINS:] * (0.1 / BINS)
     scale = lax.rsqrt(floor + 1e-06)
     first = lax.broadcasted_iota(jnp.int32, re.shape, 1) == 0
@@ -76,47 +84,57 @@
 
 
 GROUP = 8
+PIECES = 4
 END = SEG_LEN + LANES
 
 
-def spectra_kernel(x_hbm, table_hbm, re_ref, im_ref, ends_ref, x_ref, table_ref, sems):
+def spectra_kernel(x_hbm, table_hbm, re_ref, im_ref, head_ref, x_ref, table_ref, sems):
     rows, span = x_ref.shape
     segs = span // SEG_LEN
-    width = GROUP * SEG_LEN
-    groups = span // width
+    width = span // PIECES
     copies = [
         pltpu.make_async_copy(
             x_hbm.at[:, g * width : (g + 1) * width],
             x_ref.at[:, g * width : (g + 1) * width],
             sems.at[g],
         )
-        for g in range(groups)
+        for g in range(PIECES)
     ]
-    table_copy = pltpu.make_async_copy(table_hbm, table_ref, sems.at[groups])
+    table_copy = pltpu.make_async_copy(table_hbm, table_ref, sems.at[PIECES])
     copies[0].start()
     table_copy.start()
     for copy in copies[1:]:
         copy.start()
-    copies[0].wait()
+    arrived = 0
     table_copy.wait()
-    nothing = jnp.zeros((rows, LANES), F32)
-    for g in range(groups):
-        if g + 1 < groups:
-            copies[g + 1].wait()
-        own, rim = [], []
-        for s in range(g * GROUP, (g + 1) * GROUP):
-            start = s * SEG_LEN
-            stop = start + SEG_LEN
-            own.append(x_ref[:, start:stop])
-            left = x_ref[:, start - LANES : start] if s > 0 else nothing
-            right = x_ref[:, stop : stop + LANES] if s < segs - 1 else nothing
-            rim.append(beside(right, left))
-        re, im = whiten(jnp.concatenate(own, axis=0), jnp.concatenate(rim, axis=0), table_ref)
-        at = slice(g * GROUP * rows, (g + 1) * GROUP * rows)
-        re_ref[at, :] = re
-        im_ref[at, :] = im
-    ends_ref[:, :END] = x_ref[:, :END]
-    ends_ref[:, END:] = x_ref[:, span - END :]
+    starts = list(range(1, segs - 1, GROUP))
+    normed, spec = {}, {}
+    for g in range(len(starts) + 2):
+        if g < len(starts):
+            own, rim = [], []
+            stop = min(starts[g] + GROUP, segs - 1)
+            while arrived * width < stop * SEG_LEN + LANES:
+                for copy in copies[arrived : arrived + 2]:
+                    copy.wait()
+                arrived += 2
+            for s in range(starts[g], stop):
+                first, last = s * SEG_LEN, (s + 1) * SEG_LEN
+                own.append(x_ref[:, first:last])
+                rim.append(
+                    beside(x_ref[:, last : last + LANES], x_ref[:, first - LANES : first])
+                )
+            normed[g] = level(
+                jnp.concatenate(own, axis=0), jnp.concatenate(rim, axis=0), table_ref
+            )
+        if 0 <= g - 1 < len(starts):
+            spec[g - 1] = transform(*normed.pop(g - 1), table_ref)
+        if 0 <= g - 2:
+            re, im = whiten(*spec.pop(g - 2), table_ref)
+            first = (starts[g - 2] + 1) * rows
+            at = slice(first, first + re.shape[0])
+            re_ref[at, :] = re
+            im_ref[at, :] = im
+    head_ref[...] = x_ref[:, :END]
 
 
 def spectra(traces, table):
@@ -125,13 +143,13 @@
     half = jax.ShapeDtypeStruct((segs * rows, BINS), F32)
     return pl.pallas_call(
         spectra_kernel,
-        out_shape=(half, half, jax.ShapeDtypeStruct((rows, 2 * END), F32)),
+        out_shape=(half, half, jax.ShapeDtypeStruct((rows, END), F32)),
         in_specs=[pl.BlockSpec(memory_space=pltpu.HBM)] * 2,
         out_specs=(VMEM, VMEM, VMEM),
         scratch_shapes=[
             pltpu.VMEM(traces.shape, F32),
             pltpu.VMEM(table.shape, BF16),
-            pltpu.SemaphoreType.DMA((span // (GROUP * SEG_LEN) + 1,)),
+            pltpu.SemaphoreType.DMA((PIECES + 1,)),
         ],
         compiler_params=pltpu.CompilerParams(vmem_limit_bytes=32 << 20),
         name="spectra",
@@ -142,53 +160,60 @@
 
 
 def turn_kernel(
-    re_ref, im_ref, ends_ref, before_ref, after_ref, live_ref, valid_ref, table_ref,
-    out_ref, turned_ref,
+    re_ref, im_ref, head_ref, before_ref, live_ref, valid_ref, table_ref, out_ref, turned_ref
 ):
-    rows = ends_ref.shape[0]
+    rows = head_ref.shape[0]
     segs = re_ref.shape[0] // rows
-    x = jnp.concatenate([ends_ref[:, :SEG_LEN], ends_ref[:, END + LANES :]], axis=0)
+    joined = jnp.where(lax.axis_index("tm") > 0, 1.0, 0.0)
+    x = jnp.concatenate([before_ref[:, LANES:END], head_ref[:, :SEG_LEN]], axis=0)
     rim = [
-        beside(ends_ref[:, SEG_LEN:END], before_ref[...]),
-        beside(after_ref[...], ends_ref[:, END : END + LANES]),
+        beside(head_ref[:, :LANES] * joined, before_ref[:, :LANES]),
+        beside(head_ref[:, SEG_LEN:END], before_ref[:, SEG_LEN:END] * joined),
     ]
-    fixed = whiten(x, jnp.concatenate(rim, axis=0), table_ref)
+    fixed = level(x, jnp.concatenate(rim, axis=0), table_ref)
+    fixed = whiten(*transform(*fixed, table_ref), table_ref)
     row = lax.broadcasted_iota(jnp.int32, (8, BINS), 0)
     for c in range(rows):
         pieces = []
         for ref, ends in zip((re_ref, im_ref), fixed):
             picked = ref[pl.ds(c, segs, stride=rows), :]
-            pieces += [
-                jnp.where(row == 0, ends[c : c + 1], picked[:8]),
-                picked[8 : segs - 8],
-                jnp.where(row == 7, ends[rows + c : rows + c + 1], picked[segs - 8 :]),
-            ]
+            top = jnp.where(row == 1, ends[rows + c : rows + c + 1], picked[:8])
+            pieces += [jnp.where(row == 0, ends[c : c + 1], top), picked[8:]]
         turned_ref[pl.ds(c, BINS, stride=rows), :] = jnp.concatenate(pieces, axis=0).T
     live = jnp.broadcast_to(live_ref[...].astype(F32), (rows, rows))
     here = [lax.broadcasted_iota(jnp.int32, (rows, rows), axis) for axis in range(2)]
     live = jnp.sum(jnp.where(here[0] == here[1], live, 0.0), axis=1, keepdims=True)
-    mask = live * valid_ref[...].astype(F32)
-    mask = jnp.concatenate([mask, mask], axis=1)
+    valid = valid_ref[...].astype(F32)
+    valid = jnp.concatenate([valid, valid], axis=1)
+    lane = lax.broadcasted_iota(jnp.int32, valid.shape, 1)
+    other = before_ref[:, :LANES]
+    other = jnp.where(lane < segs, other, pltpu.roll(other, segs, 1))
+    mask = live * pltpu.roll(jnp.where(lane % segs == segs - 1, other, valid), 1, 1)
     whitened = turned_ref[...].reshape(BINS, rows, LANES) * mask[None]
     out_ref[...] = whitened.astype(BF16)
 
 
-def turn(parts, before, after, live, valid, table):
+def turn(parts, before, live, valid, table):
     rows, segs = valid.shape
     return pl.pallas_call(
         turn_kernel,
         out_shape=jax.ShapeDtypeStruct((BINS, rows, 2 * segs), BF16),
-        in_specs=[VMEM] * 8,
+        in_specs=[VMEM] * 7,
         out_specs=VMEM,
         scratch_shapes=[pltpu.VMEM((BINS * rows, LANES), F32)],
         compiler_params=pltpu.CompilerParams(vmem_limit_bytes=32 << 20),
         name="turn",
-    )(*parts, before, after, live[None, :], valid, table)
-
-
-def front(traces, before, after, live, valid):
+    )(*parts, before, live[None, :], valid, table)
+
+
+def front(traces, live, valid):
+    slabs, span = lax.axis_size("tm"), traces.shape[1]
+    tail = traces[:, span - END :]
+    bits = jnp.pad(valid, ((0, 0), (0, END - valid.shape[1]))).astype(F32)
+    tail = jnp.where(lax.broadcasted_iota(jnp.int32, tail.shape, 1) < valid.shape[1], bits, tail)
+    before = lax.ppermute(tail, "tm", [(i, (i + 1) % slabs) for i in range(slabs)])
     table = jnp.asarray(front_tables())
-    return turn(spectra(traces, table), before, after, live, valid, table)
+    return turn(spectra(traces, table), before, live, valid, table)
 
 
 def cross_kernel(got_ref, out_ref, x_ref, r_ref):
@@ -243,13 +268,8 @@
 
 
 def body(traces, live_channel, valid_segment):
-    span = traces.shape[1]
     chans, slabs = lax.axis_size("chan"), lax.axis_size("tm")
-    up = [(i, i + 1) for i in range(slabs - 1)]
-    down = [(j, i) for i, j in up]
-    before = lax.ppermute(traces[:, span - LANES :], "tm", up)
-    after = lax.ppermute(traces[:, :LANES], "tm", down)
-    sent = front(traces, before, after, live_channel, valid_segment)
+    sent = front(traces, live_channel, valid_segment)
     got = lax.all_to_all(sent, ALL, 0, 0, tiled=True)
     pieces = cross_spectra(got.reshape(chans, slabs, *got.shape[1:]))
     back = lax.all_to_all(pieces.reshape(got.shape), ALL, 0, 0, tiled=True)

time: 78.8 us -> 69.4 us (0.88)
  starting transfers between devices: 5.94 us -> 2.19 us
  Pallas kernels: 12.3 us -> 9.33 us
  blocking collectives: 55.2 us -> 52.5 us
  other arithmetic: 0.6 us -> 1.48 us
  local copies, waits for them, and re-layouts: 2.12 us -> 1.31 us
    ppermute x2 -> x1, starting transfers between devices: 5.94 us -> 2.19 us  [front(): lax.ppermute(tail, 'tm', [(i, (i + 1) % slabs) for i in range(slabs)])]
    pallas_call x1, Pallas kernels: 7.08 us -> 4.05 us  [spectra(): pl.pallas_call(spectra_kernel, out_shape=(half, half, jax.ShapeDtypeStruc...]
    all_to_all x1, blocking collectives: 31.9 us -> 29.3 us  [body(): got = lax.all_to_all(sent, ALL, 0, 0, tiled=True)]
    select_n x0 -> x1, other arithmetic: none -> 0.87 us  [front(): jnp.where(lax.broadcasted_iota(jnp.int32, tail.shape, 1) < valid.shape[1]...]
    slice x1 -> x0, local copies, waits for them, and re-layouts: 0.8 us -> none  [body(): after = lax.ppermute(traces[:, :LANES], 'tm', down)]
  transfers between devices with their start and end apart: 2 -> 1, of which waited for: 0 -> 0; matrix products, arithmetic and copies ran while one was open for 0% -> 0% of each run, Pallas kernels for 9% -> 6%
where the time goes in v4:
time: 69.4 us; the launch traced here: 69.2 us
  blocking collectives  52.5 us (76%)
  Pallas kernels  9.33 us (13%)
  matrix products  2.33 us (3%)
  starting transfers between devices  2.19 us (3%)
  other arithmetic  1.48 us (2%)
  local copies, waits for them, and re-layouts  1.31 us (2%)
    all_to_all x1, blocking collectives, body(): got = lax.all_to_all(sent, ALL, 0, 0, tiled=True)  29.3 us
    all_to_all x1, blocking collectives, body(): back = lax.all_to_all(pieces.reshape(got.shape), ALL, 0, 0, tiled=True)  23.2 us
    pallas_call x1, Pallas kernels, spectra(): pl.pallas_call(spectra_kernel, out_shape=(half, half, jax.ShapeDtypeStruc...  4.05 us
    pallas_call x1, Pallas kernels, turn(): pl.pallas_call(turn_kernel, out_shape=jax.ShapeDtypeStruct((BINS, rows, 2...  3.23 us
    dot_general x1, matrix products, body(): jnp.einsum('fikj,fkl->ijl', back, jnp.asarray(inverse_tables()), precisio...  2.33 us
    ppermute x1, starting transfers between devices, front(): lax.ppermute(tail, 'tm', [(i, (i + 1) % slabs) for i in range(slabs)])  2.19 us
    pallas_call x1, Pallas kernels, cross_spectra(): pl.pallas_call(cross_kernel, out_shape=jax.ShapeDtypeStruct(got.shape, BF...  2.05 us
  transfers between devices with their start and end apart: 1, of which 0 were waited for; matrix products, arithmetic and copies ran while one was open for 0% of the time, Pallas kernels for 6%

profile of v4, /device:TPU:1, one launch (start us, length us, event | category | flops | bytes accessed | tf_op | source)
XLA Modules:
  0.0 69.2 jit_solution(1167387403592350915)
XLA Ops:
  0.0 0.0 copy-start
  0.0 0.0 copy-start.1
  0.0 0.0 copy-start.2
  0.0 0.9 %slice_select_fusion = f32[32,384]{1,0:T(8,128)S(1)} fusion(f32[32,16384]{1,0:T(8,128)} %x_hbm.1, s32[32,64]{1,0:T(8,128)} %valid_ref.1, pred[384]{0:T(512)(128)(4,1)S(1)} %iota_compare_fusion), kind=kLoop, calls=%fused_computation.5 | loop fusion | flops 24576 | bytes 106880 | tf_op jit(solution)/shard_map/jit(_where)/select_n | solution.py:213
  0.9 2.2 %collective-permute-start = (f32[32,384]{1,0:T(8,128)S(1)}, f32[32,384]{1,0:T(8,128)S(1)}, u32[]{:S(2)}, u32[]{:S(2)}) collective-permute-start(f32[32,384]{1,0:T(8,128)S(1)} %slice_select_fusion), channel_id=1, source_target_pairs={{0,1},{1,2},{2,3},{3,4},{4,5},{5,6},{6,7},{7,0},{8,9},{9,10},{10,1... | collective-permute-start | bytes 147464 | tf_op jit(solution)/shard_map/ppermute | solution.py:214
  3.1 4.1 %spectra.1 = (f32[2048,128]{1,0:T(8,128)S(1)}, f32[2048,128]{1,0:T(8,128)S(1)}, f32[32,384]{1,0:T(8,128)S(1)}) custom-call(f32[32,16384]{1,0:T(8,128)} %x_hbm.1, bf16[5,256,256]{2,1,0:T(8,128)(2,1)} %constant.12.clone.table_hbm.table_ref), custom_call_target="tpu_custom_call" | custom-call | tf_op jit(solution)/shard_map/spectra/pallas_call | solution.py:144
  7.1 0.0 collective-permute-done.before_ref
  7.2 0.0 copy-done
  7.2 0.0 copy-done.1
  7.2 0.0 copy-done.2
  7.2 3.2 %turn.1 = bf16[128,32,128]{2,1,0:T(8,128)(2,1)S(1)} custom-call(f32[2048,128]{1,0:T(8,128)S(1)} %get-tuple-element.8.re_ref, f32[2048,128]{1,0:T(8,128)S(1)} %get-tuple-element.9.im_ref, f32[32,384]{1,0:T(8,128)S(1)} %get-tuple-element.10.head_ref, f32[32,384]{1,0:T(8,128)S(1)} %collective-permute-done.before_ref, s32[1,32]{1,0:T(1,128)S(1)} %bitcast.13, ...), custom_call_target="tpu_custom_call" | custom-call | tf_op jit(solution)/shard_map/turn/pallas_call | solution.py:198
  10.4 29.3 %all_to_all.10 = bf16[128,32,128]{2,1,0:T(8,128)(2,1)S(1)} all-to-all(bf16[128,32,128]{2,1,0:T(8,128)(2,1)S(1)} %turn.1), channel_id=1, replica_groups=mesh['chan'=16,'tm'=8] {'chan','tm'}, dimensions={0} | all-to-all | bytes 2097152 | tf_op jit(solution)/shard_map/all_to_all | solution.py:273
  39.7 2.0 %cross_spectra.1 = bf16[16,8,32,128]{3,2,1,0:T(8,128)(2,1)S(1)} custom-call(bf16[16,8,32,128]{3,2,1,0:T(8,128)(2,1)S(1)} %bitcast.11), custom_call_target="tpu_custom_call" | custom-call | tf_op jit(solution)/shard_map/cross_spectra/pallas_call | solution.py:256
  41.7 23.2 %all_to_all.11 = bf16[128,32,128]{2,1,0:T(8,128)(2,1)S(1)} all-to-all(bf16[128,32,128]{2,1,0:T(8,128)(2,1)S(1)} %bitcast.12), channel_id=1, replica_groups=mesh['chan'=16,'tm'=8] {'chan','tm'}, dimensions={0} | all-to-all | bytes 2097152 | tf_op jit(solution)/shard_map/all_to_all | solution.py:275
  65.0 1.0 %copy.7 = bf16[128,32,128]{0,2,1:T(8,128)(2,1)S(1)} copy(bf16[128,32,128]{2,1,0:T(8,128)(2,1)S(1)} %all_to_all.11) | data formatting | bytes 2097152 | tf_op jit(solution)/shard_map/all_to_all | solution.py:275
  65.9 0.0 copy-start.3
  66.0 0.2 bitcast_convert_fusion
  66.2 0.4 fusion.2
  66.6 0.3 copy-done.3
  66.9 2.3 %bitcast_multiply_fusion = f32[32,64,256]{2,1,0:T(8,128)} fusion(bf16[128,32,2,64]{0,3,2,1:T(8,128)(2,1)S(1)} %bitcast.14, f32[128,2,256,1]{2,0,1,3:T(8,128)S(1)} %copy-done.3, f32[32,64]{1,0:T(8,128)S(1)} %fusion.2), kind=kOutput, calls=%fused_computation | convolution fusion | flops 1611137024 | bytes 3416064 | tf_op jit(solution)/shard_map/fikj,fkl->ijl/dot_general | solution.py:279
  (1 shorter events, 0.0 us)
Async XLA Ops:
  0.0 7.2 %copy-start = (bf16[5,256,256]{2,1,0:T(8,128)(2,1)S(1)}, bf16[5,256,256]{2,1,0:T(8,128)(2,1)}, u32[]{:S(2)}) copy-start(bf16[5,256,256]{2,1,0:T(8,128)(2,1)} %constant.12.clone.table_hbm.table_ref) | copy-start | bytes 1966084
  0.0 7.2 %copy-start.1 = (s32[32,64]{1,0:T(8,128)S(1)}, s32[32,64]{1,0:T(8,128)}, u32[]{:S(2)}) copy-start(s32[32,64]{1,0:T(8,128)} %valid_ref.1) | copy-start | bytes 24580
  0.0 7.2 %copy-start.2 = (s32[32]{0:T(128)S(1)}, s32[32]{0:T(128)}, u32[]{:S(2)}) copy-start(s32[32]{0:T(128)} %param.6) | copy-start | bytes 388
  0.9 6.3 %collective-permute-start = (f32[32,384]{1,0:T(8,128)S(1)}, f32[32,384]{1,0:T(8,128)S(1)}, u32[]{:S(2)}, u32[]{:S(2)}) collective-permute-start(f32[32,384]{1,0:T(8,128)S(1)} %slice_select_fusion), channel_id=1, source_target_pairs={{0,1},{1,2},{2,3},{3,4},{4,5},{5,6},{6,7},{7,0},{8,9},{9,10},{10,1... | collective-permute-start | bytes 147464 | tf_op jit(solution)/shard_map/ppermute | solution.py:214
  65.9 1.0 %copy-start.3 = (f32[128,2,256,1]{2,0,1,3:T(8,128)S(1)}, f32[128,2,256,1]{2,0,1,3:T(8,128)}, u32[]{:S(2)}) copy-start(f32[128,2,256,1]{2,0,1,3:T(8,128)} %constant.16) | copy-start | bytes 786436

commit v5 on v4

--- a/solution.py
+++ b/solution.py
@@ -38,12 +38,14 @@
     return np.stack([box_mid, np.tile(box_edge, (2, 1)), *split(forward), np.tile(band, (2, 1))])
 
 
-def inverse_tables():
+def inverse_table():
     freq = np.arange(BINS)[:, None]
     lag = np.arange(SEG_LEN)[None, :] - BINS
     phase = 2.0 * np.pi / SEG_LEN * (freq * lag % SEG_LEN)
-    table = np.stack([np.cos(phase), -np.sin(phase)], axis=1) * (freq > 0)[:, None, :]
-    return table.astype(np.float32)
+    table = np.concatenate([np.cos(phase), -np.sin(phase)], axis=0).astype(np.float32)
+    table = table * np.tile(freq > 0, (2, 1))
+    count = np.broadcast_to(np.tile(freq == 0, (2, 1)), (2 * BINS, LANES)).astype(BF16)
+    return np.concatenate([*split(table), count], axis=1)
 
 
 def mxu(a, b):
@@ -85,6 +87,7 @@
 
 GROUP = 8
 PIECES = 4
+PAD = 4
 END = SEG_LEN + LANES
 
 
@@ -130,17 +133,17 @@
             spec[g - 1] = transform(*normed.pop(g - 1), table_ref)
         if 0 <= g - 2:
             re, im = whiten(*spec.pop(g - 2), table_ref)
-            first = (starts[g - 2] + 1) * rows
-            at = slice(first, first + re.shape[0])
-            re_ref[at, :] = re
-            im_ref[at, :] = im
+            for s in range(re.shape[0] // rows):
+                first = (starts[g - 2] + 1 + s) * (rows + PAD)
+                re_ref[first : first + rows, :] = re[s * rows : (s + 1) * rows]
+                im_ref[first : first + rows, :] = im[s * rows : (s + 1) * rows]
     head_ref[...] = x_ref[:, :END]
 
 
 def spectra(traces, table):
     rows, span = traces.shape
     segs = span // SEG_LEN
-    half = jax.ShapeDtypeStruct((segs * rows, BINS), F32)
+    half = jax.ShapeDtypeStruct((segs * (rows + PAD), BINS), F32)
     return pl.pallas_call(
         spectra_kernel,
         out_shape=(half, half, jax.ShapeDtypeStruct((rows, END), F32)),
@@ -163,7 +166,7 @@
     re_ref, im_ref, head_ref, before_ref, live_ref, valid_ref, table_ref, out_ref, turned_ref
 ):
     rows = head_ref.shape[0]
-    segs = re_ref.shape[0] // rows
+    segs = valid_ref.shape[1]
     joined = jnp.where(lax.axis_index("tm") > 0, 1.0, 0.0)
     x = jnp.concatenate([before_ref[:, LANES:END], head_ref[:, :SEG_LEN]], axis=0)
     rim = [
@@ -176,10 +179,10 @@
     for c in range(rows):
         pieces = []
         for ref, ends in zip((re_ref, im_ref), fixed):
-            picked = ref[pl.ds(c, segs, stride=rows), :]
+            picked = ref[pl.ds(c, segs, stride=rows + PAD), :]
             top = jnp.where(row == 1, ends[rows + c : rows + c + 1], picked[:8])
             pieces += [jnp.where(row == 0, ends[c : c + 1], top), picked[8:]]
-        turned_ref[pl.ds(c, BINS, stride=rows), :] = jnp.concatenate(pieces, axis=0).T
+        turned_ref[pl.ds(c, BINS, stride=rows + PAD), :] = jnp.concatenate(pieces, axis=0).T
     live = jnp.broadcast_to(live_ref[...].astype(F32), (rows, rows))
     here = [lax.broadcasted_iota(jnp.int32, (rows, rows), axis) for axis in range(2)]
     live = jnp.sum(jnp.where(here[0] == here[1], live, 0.0), axis=1, keepdims=True)
@@ -189,8 +192,9 @@
     other = before_ref[:, :LANES]
     other = jnp.where(lane < segs, other, pltpu.roll(other, segs, 1))
     mask = live * pltpu.roll(jnp.where(lane % segs == segs - 1, other, valid), 1, 1)
-    whitened = turned_ref[...].reshape(BINS, rows, LANES) * mask[None]
-    out_ref[...] = whitened.astype(BF16)
+    for f in range(BINS):
+        first = f * (rows + PAD)
+        out_ref[f] = (turned_ref[first : first + rows, :] * mask).astype(BF16)
 
 
 def turn(parts, before, live, valid, table):
@@ -200,7 +204,7 @@
         out_shape=jax.ShapeDtypeStruct((BINS, rows, 2 * segs), BF16),
         in_specs=[VMEM] * 7,
         out_specs=VMEM,
-        scratch_shapes=[pltpu.VMEM((BINS * rows, LANES), F32)],
+        scratch_shapes=[pltpu.VMEM((BINS * (rows + PAD), LANES), F32)],
         compiler_params=pltpu.CompilerParams(vmem_limit_bytes=32 << 20),
         name="turn",
     )(*parts, before, live[None, :], valid, table)
@@ -267,23 +271,59 @@
     )(got)
 
 
+def inverse_kernel(back_ref, table_ref, out_hbm, turned_ref, out_ref, sems):
+    _, rows, lanes = back_ref.shape
+    cols = lanes // 2
+    for f in range(BINS):
+        turned_ref[f * (rows + PAD) : f * (rows + PAD) + rows, :] = back_ref[f].astype(F32)
+    groups = rows // GROUP
+    pieces = {}
+    copies = []
+    for g in range(groups + 1):
+        if g < groups:
+            piece = []
+            for i in range(g * GROUP, (g + 1) * GROUP):
+                turned = turned_ref[pl.ds(i, BINS, stride=rows + PAD), :].T.astype(BF16)
+                piece.append(jnp.concatenate([turned[:cols], turned[cols:]], axis=1))
+            pieces[g] = jnp.concatenate(piece, axis=0)
+        if g > 0:
+            full = mxu(pieces.pop(g - 1), table_ref[...])
+            scale = 2.0 / jnp.maximum(full[:, 2 * SEG_LEN :], 1.0)
+            lagged = full[:, :SEG_LEN] + full[:, SEG_LEN : 2 * SEG_LEN]
+            lagged = lagged * jnp.concatenate([scale, scale], axis=1)
+            at = slice((g - 1) * GROUP, g * GROUP)
+            out_ref[at] = lagged.reshape(GROUP, cols, SEG_LEN)
+            copies.append(pltpu.make_async_copy(out_ref.at[at], out_hbm.at[at], sems.at[g - 1]))
+            copies[-1].start()
+    for copy in copies:
+        copy.wait()
+
+
+def inverse(back):
+    bins, rows, lanes = back.shape
+    shape = (rows, lanes // 2, SEG_LEN)
+    return pl.pallas_call(
+        inverse_kernel,
+        out_shape=jax.ShapeDtypeStruct(shape, F32),
+        in_specs=[VMEM, VMEM],
+        out_specs=pl.BlockSpec(memory_space=pltpu.HBM),
+        scratch_shapes=[
+            pltpu.VMEM((bins * (rows + PAD), lanes), F32),
+            pltpu.VMEM(shape, F32),
+            pltpu.SemaphoreType.DMA((rows // GROUP,)),
+        ],
+        compiler_params=pltpu.CompilerParams(vmem_limit_bytes=32 << 20),
+        name="inverse",
+    )(back, jnp.asarray(inverse_table()))
+
+
 def body(traces, live_channel, valid_segment):
     chans, slabs = lax.axis_size("chan"), lax.axis_size("tm")
     sent = front(traces, live_channel, valid_segment)
     got = lax.all_to_all(sent, ALL, 0, 0, tiled=True)
     pieces = cross_spectra(got.reshape(chans, slabs, *got.shape[1:]))
     back = lax.all_to_all(pieces.reshape(got.shape), ALL, 0, 0, tiled=True)
-    rows, cols = back.shape[1], back.shape[2] // 2
-    back = back.reshape(BINS, rows, 2, cols).astype(F32)
-    count = back[0, :, 0] + back[0, :, 1]
-    lagged = jnp.einsum(
-        "fikj,fkl->ijl",
-        back,
-        jnp.asarray(inverse_tables()),
-        precision=lax.Precision.HIGHEST,
-        preferred_element_type=F32,
-    )
-    return lagged * (2.0 / jnp.maximum(count, 1.0))[:, :, None]
+    return inverse(back)
 
 
 def solution(mesh):

time: 69.4 us -> 65.2 us (0.939)
  matrix products: 2.33 us -> 0 us
  local copies, waits for them, and re-layouts: 1.31 us -> 0.01 us
    dot_general x1 -> x0, matrix products: 2.33 us -> none  [body(): jnp.einsum('fikj,fkl->ijl', back, jnp.asarray(inverse_tables()), precisio...]
    pallas_call x0 -> x1, Pallas kernels: none -> 1.96 us  [inverse(): pl.pallas_call(inverse_kernel, out_shape=jax.ShapeDtypeStruct(shape, F32)...]
    pallas_call x1, Pallas kernels: 3.23 us -> 1.35 us  [turn(): pl.pallas_call(turn_kernel, out_shape=jax.ShapeDtypeStruct((BINS, rows, 2...]
    all_to_all x1 -> x0, local copies, waits for them, and re-layouts: 0.97 us -> none  [body(): back = lax.all_to_all(pieces.reshape(got.shape), ALL, 0, 0, tiled=True)]
where the time goes in v5:
time: 65.2 us; the launch traced here: 65.1 us
  blocking collectives  52.5 us (81%)
  Pallas kernels  9.41 us (14%)
  starting transfers between devices  2.19 us (3%)
  other arithmetic  0.88 us (1%)
    all_to_all x1, blocking collectives, body(): got = lax.all_to_all(sent, ALL, 0, 0, tiled=True)  29.3 us
    all_to_all x1, blocking collectives, body(): back = lax.all_to_all(pieces.reshape(got.shape), ALL, 0, 0, tiled=True)  23.2 us
    pallas_call x1, Pallas kernels, spectra(): pl.pallas_call(spectra_kernel, out_shape=(half, half, jax.ShapeDtypeStruc...  4.05 us
    ppermute x1, starting transfers between devices, front(): lax.ppermute(tail, 'tm', [(i, (i + 1) % slabs) for i in range(slabs)])  2.19 us
    pallas_call x1, Pallas kernels, cross_spectra(): pl.pallas_call(cross_kernel, out_shape=jax.ShapeDtypeStruct(got.shape, BF...  2.05 us
    pallas_call x1, Pallas kernels, inverse(): pl.pallas_call(inverse_kernel, out_shape=jax.ShapeDtypeStruct(shape, F32)...  1.96 us
    pallas_call x1, Pallas kernels, turn(): pl.pallas_call(turn_kernel, out_shape=jax.ShapeDtypeStruct((BINS, rows, 2...  1.35 us
  transfers between devices with their start and end apart: 1, of which 0 were waited for; matrix products, arithmetic and copies ran while one was open for 0% of the time, Pallas kernels for 6%

profile of v5, /device:TPU:1, one launch (start us, length us, event | category | flops | bytes accessed | tf_op | source)
XLA Modules:
  0.0 65.1 jit_solution(5525620993962440488)
XLA Ops:
  0.0 0.0 copy-start
  0.0 0.0 copy-start.2
  0.0 0.0 copy-start.3
  0.0 0.9 %slice_select_fusion = f32[32,384]{1,0:T(8,128)S(1)} fusion(f32[32,16384]{1,0:T(8,128)} %x_hbm.1, s32[32,64]{1,0:T(8,128)} %valid_ref.1, pred[384]{0:T(512)(128)(4,1)S(1)} %iota_compare_fusion), kind=kLoop, calls=%fused_computation | loop fusion | flops 24576 | bytes 106880 | tf_op jit(solution)/shard_map/jit(_where)/select_n | solution.py:217
  0.9 2.2 %collective-permute-start = (f32[32,384]{1,0:T(8,128)S(1)}, f32[32,384]{1,0:T(8,128)S(1)}, u32[]{:S(2)}, u32[]{:S(2)}) collective-permute-start(f32[32,384]{1,0:T(8,128)S(1)} %slice_select_fusion), channel_id=1, source_target_pairs={{0,1},{1,2},{2,3},{3,4},{4,5},{5,6},{6,7},{7,0},{8,9},{9,10},{10,1... | collective-permute-start | bytes 147464 | tf_op jit(solution)/shard_map/ppermute | solution.py:218
  3.1 4.1 %spectra.1 = (f32[2304,128]{1,0:T(8,128)S(1)}, f32[2304,128]{1,0:T(8,128)S(1)}, f32[32,384]{1,0:T(8,128)S(1)}) custom-call(f32[32,16384]{1,0:T(8,128)} %x_hbm.1, bf16[5,256,256]{2,1,0:T(8,128)(2,1)} %constant.8.clone.table_hbm.table_ref), custom_call_target="tpu_custom_call" | custom-call | tf_op jit(solution)/shard_map/spectra/pallas_call | solution.py:147
  7.1 0.0 collective-permute-done.before_ref
  7.2 0.0 copy-done
  7.2 0.0 copy-done.2
  7.2 0.0 copy-done.3
  7.2 1.3 %turn.1 = bf16[128,32,128]{2,1,0:T(8,128)(2,1)S(1)} custom-call(f32[2304,128]{1,0:T(8,128)S(1)} %get-tuple-element.8.re_ref, f32[2304,128]{1,0:T(8,128)S(1)} %get-tuple-element.9.im_ref, f32[32,384]{1,0:T(8,128)S(1)} %get-tuple-element.10.head_ref, f32[32,384]{1,0:T(8,128)S(1)} %collective-permute-done.before_ref, s32[1,32]{1,0:T(1,128)S(1)} %bitcast.5, ...), custom_call_target="tpu_custom_call" | custom-call | tf_op jit(solution)/shard_map/turn/pallas_call | solution.py:202
  8.5 29.3 %all_to_all.10 = bf16[128,32,128]{2,1,0:T(8,128)(2,1)S(1)} all-to-all(bf16[128,32,128]{2,1,0:T(8,128)(2,1)S(1)} %turn.1), channel_id=1, replica_groups=mesh['chan'=16,'tm'=8] {'chan','tm'}, dimensions={0} | all-to-all | bytes 2097152 | tf_op jit(solution)/shard_map/all_to_all | solution.py:323
  37.8 0.0 copy-start.1
  37.8 2.0 %cross_spectra.1 = bf16[16,8,32,128]{3,2,1,0:T(8,128)(2,1)S(1)} custom-call(bf16[16,8,32,128]{3,2,1,0:T(8,128)(2,1)S(1)} %bitcast.3), custom_call_target="tpu_custom_call" | custom-call | tf_op jit(solution)/shard_map/cross_spectra/pallas_call | solution.py:260
  39.9 23.2 %all_to_all.11.back_ref = bf16[128,32,128]{2,1,0:T(8,128)(2,1)S(1)} all-to-all(bf16[128,32,128]{2,1,0:T(8,128)(2,1)S(1)} %bitcast.4), channel_id=1, replica_groups=mesh['chan'=16,'tm'=8] {'chan','tm'}, dimensions={0} | all-to-all | bytes 2097152 | tf_op jit(solution)/shard_map/all_to_all | solution.py:325
  63.1 0.0 copy-done.1
  63.1 2.0 %inverse.1 = f32[32,64,256]{2,1,0:T(8,128)} custom-call(bf16[128,32,128]{2,1,0:T(8,128)(2,1)S(1)} %all_to_all.11.back_ref, bf16[256,640]{1,0:T(8,128)(2,1)S(1)} %copy-done.1), custom_call_target="tpu_custom_call" | custom-call | tf_op jit(solution)/shard_map/inverse/pallas_call | solution.py:305
  (1 shorter events, 0.0 us)
Async XLA Ops:
  0.0 7.2 %copy-start = (bf16[5,256,256]{2,1,0:T(8,128)(2,1)S(1)}, bf16[5,256,256]{2,1,0:T(8,128)(2,1)}, u32[]{:S(2)}) copy-start(bf16[5,256,256]{2,1,0:T(8,128)(2,1)} %constant.8.clone.table_hbm.table_ref) | copy-start | bytes 1966084
  0.0 7.2 %copy-start.2 = (s32[32,64]{1,0:T(8,128)S(1)}, s32[32,64]{1,0:T(8,128)}, u32[]{:S(2)}) copy-start(s32[32,64]{1,0:T(8,128)} %valid_ref.1) | copy-start | bytes 24580
  0.0 7.2 %copy-start.3 = (s32[32]{0:T(128)S(1)}, s32[32]{0:T(128)}, u32[]{:S(2)}) copy-start(s32[32]{0:T(128)} %param.6) | copy-start | bytes 388
  0.9 6.3 %collective-permute-start = (f32[32,384]{1,0:T(8,128)S(1)}, f32[32,384]{1,0:T(8,128)S(1)}, u32[]{:S(2)}, u32[]{:S(2)}) collective-permute-start(f32[32,384]{1,0:T(8,128)S(1)} %slice_select_fusion), channel_id=1, source_target_pairs={{0,1},{1,2},{2,3},{3,4},{4,5},{5,6},{6,7},{7,0},{8,9},{9,10},{10,1... | collective-permute-start | bytes 147464 | tf_op jit(solution)/shard_map/ppermute | solution.py:218
  37.8 25.3 %copy-start.1 = (bf16[256,640]{1,0:T(8,128)(2,1)S(1)}, bf16[256,640]{1,0:T(8,128)(2,1)}, u32[]{:S(2)}) copy-start(bf16[256,640]{1,0:T(8,128)(2,1)} %constant.9.clone.table_ref) | copy-start | bytes 983044

commit v6 on v5

--- a/solution.py
+++ b/solution.py
@@ -223,36 +223,38 @@
 def cross_kernel(got_ref, out_ref, x_ref, r_ref):
     chans, slabs, rows, _ = got_ref.shape
     cols = chans * rows // slabs
+    blocks = chans // slabs
     half = LANES // 2
-    lane = lax.broadcasted_iota(jnp.int32, (chans * rows, LANES), 1)
-    sign = jnp.where(lane < half, 1.0, -1.0)
+    counts = lax.axis_index("chan") * lax.axis_size("tm") + lax.axis_index("tm") == 0
+    kept = jnp.where(counts, 0.0, 1.0)
+    lane = lax.broadcasted_iota(jnp.int32, (cols, LANES), 1)
+    sign = jnp.where(lane < half, kept, -kept).astype(BF16)
+    moved = jnp.full((cols, LANES), 1.0 - kept).astype(BF16)
+    kept = jnp.full((cols, LANES), kept).astype(BF16)
     for t in range(slabs):
-        tile = got_ref[:, t].reshape(chans * rows, LANES)
-        turned = (pltpu.roll(tile.astype(F32), half, 1) * sign).astype(BF16)
         at = slice(t * LANES, (t + 1) * LANES)
-        x_ref[:, at] = tile
-        for u in range(slabs):
-            r_ref[2 * u * cols : (2 * u + 1) * cols, at] = tile[u * cols : (u + 1) * cols]
-            r_ref[(2 * u + 1) * cols : (2 * u + 2) * cols, at] = turned[u * cols : (u + 1) * cols]
-    middle = slabs // 2 * LANES
-
-    @pl.when(lax.axis_index("chan") * lax.axis_size("tm") + lax.axis_index("tm") == 0)
-    def _():
-        for u in range(slabs):
-            real = slice(2 * u * cols, (2 * u + 1) * cols)
-            imag = slice((2 * u + 1) * cols, (2 * u + 2) * cols)
-            own = slice(u * cols, (u + 1) * cols)
-            r_ref[real, middle:] = jnp.zeros((cols, slabs * LANES - middle), BF16)
-            r_ref[imag, :middle] = jnp.zeros((cols, middle), BF16)
-            r_ref[imag, middle:] = x_ref[own, middle:]
-
-    x = x_ref[...]
-    for u in range(0, slabs, 2):
-        r = r_ref[2 * u * cols : (2 * u + 4) * cols, :]
-        cross = lax.dot_general(x, r, (((1,), (1,)), ((), ())), preferred_element_type=F32)
+        x_ref[:, at] = got_ref[:, t].reshape(chans * rows, LANES)
+    for u in range(0, slabs + 2, 2):
+        for v in range(u, min(u + 2, slabs)):
+            own = slice(v * blocks, (v + 1) * blocks)
+            for t in range(slabs):
+                at = slice(t * LANES, (t + 1) * LANES)
+                tile = got_ref[own, t].reshape(cols, LANES)
+                turned = pltpu.roll(tile, half, 1) * sign
+                if t >= slabs // 2:
+                    turned = turned + tile * moved
+                    tile = tile * kept
+                r_ref[2 * v * cols : (2 * v + 1) * cols, at] = tile
+                r_ref[(2 * v + 1) * cols : (2 * v + 2) * cols, at] = turned
+        if u == 0:
+            continue
+        r = r_ref[2 * (u - 2) * cols : 2 * u * cols, :]
+        cross = lax.dot_general(
+            x_ref[...], r, (((1,), (1,)), ((), ())), preferred_element_type=F32
+        )
         for v in range(2):
             part = cross[:, v * LANES : (v + 1) * LANES]
-            out_ref[:, u + v] = part.astype(BF16).reshape(chans, rows, LANES)
+            out_ref[:, u - 2 + v] = part.astype(BF16).reshape(chans, rows, LANES)
 
 
 def cross_spectra(got):
@@ -271,18 +273,21 @@
     )(got)
 
 
+ROWS = 4
+
+
 def inverse_kernel(back_ref, table_ref, out_hbm, turned_ref, out_ref, sems):
     _, rows, lanes = back_ref.shape
     cols = lanes // 2
     for f in range(BINS):
         turned_ref[f * (rows + PAD) : f * (rows + PAD) + rows, :] = back_ref[f].astype(F32)
-    groups = rows // GROUP
+    groups = rows // ROWS
     pieces = {}
     copies = []
     for g in range(groups + 1):
         if g < groups:
             piece = []
-            for i in range(g * GROUP, (g + 1) * GROUP):
+            for i in range(g * ROWS, (g + 1) * ROWS):
                 turned = turned_ref[pl.ds(i, BINS, stride=rows + PAD), :].T.astype(BF16)
                 piece.append(jnp.concatenate([turned[:cols], turned[cols:]], axis=1))
             pieces[g] = jnp.concatenate(piece, axis=0)
@@ -291,8 +296,8 @@
             scale = 2.0 / jnp.maximum(full[:, 2 * SEG_LEN :], 1.0)
             lagged = full[:, :SEG_LEN] + full[:, SEG_LEN : 2 * SEG_LEN]
             lagged = lagged * jnp.concatenate([scale, scale], axis=1)
-            at = slice((g - 1) * GROUP, g * GROUP)
-            out_ref[at] = lagged.reshape(GROUP, cols, SEG_LEN)
+            at = slice((g - 1) * ROWS, g * ROWS)
+            out_ref[at] = lagged.reshape(ROWS, cols, SEG_LEN)
             copies.append(pltpu.make_async_copy(out_ref.at[at], out_hbm.at[at], sems.at[g - 1]))
             copies[-1].start()
     for copy in copies:
@@ -310,7 +315,7 @@
         scratch_shapes=[
             pltpu.VMEM((bins * (rows + PAD), lanes), F32),
             pltpu.VMEM(shape, F32),
-            pltpu.SemaphoreType.DMA((rows // GROUP,)),
+            pltpu.SemaphoreType.DMA((rows // ROWS,)),
         ],
         compiler_params=pltpu.CompilerParams(vmem_limit_bytes=32 << 20),
         name="inverse",

time: 65.2 us -> 64.5 us (0.989)
  Pallas kernels: 9.41 us -> 8.7 us
    pallas_call x1, Pallas kernels: 2.05 us -> 1.4 us  [cross_spectra(): pl.pallas_call(cross_kernel, out_shape=jax.ShapeDtypeStruct(got.shape, BF...]
where the time goes in v6:
time: 64.5 us; the launch traced here: 64.3 us
  blocking collectives  52.5 us (81%)
  Pallas kernels  8.7 us (13%)
  starting transfers between devices  2.19 us (3%)
  other arithmetic  0.88 us (1%)
    all_to_all x1, blocking collectives, body(): got = lax.all_to_all(sent, ALL, 0, 0, tiled=True)  29.3 us
    all_to_all x1, blocking collectives, body(): back = lax.all_to_all(pieces.reshape(got.shape), ALL, 0, 0, tiled=True)  23.2 us
    pallas_call x1, Pallas kernels, spectra(): pl.pallas_call(spectra_kernel, out_shape=(half, half, jax.ShapeDtypeStruc...  4.05 us
    ppermute x1, starting transfers between devices, front(): lax.ppermute(tail, 'tm', [(i, (i + 1) % slabs) for i in range(slabs)])  2.19 us
    pallas_call x1, Pallas kernels, inverse(): pl.pallas_call(inverse_kernel, out_shape=jax.ShapeDtypeStruct(shape, F32)...  1.9 us
    pallas_call x1, Pallas kernels, cross_spectra(): pl.pallas_call(cross_kernel, out_shape=jax.ShapeDtypeStruct(got.shape, BF...  1.4 us
    pallas_call x1, Pallas kernels, turn(): pl.pallas_call(turn_kernel, out_shape=jax.ShapeDtypeStruct((BINS, rows, 2...  1.35 us
  transfers between devices with their start and end apart: 1, of which 0 were waited for; matrix products, arithmetic and copies ran while one was open for 0% of the time, Pallas kernels for 6%

profile of v6, /device:TPU:1, one launch (start us, length us, event | category | flops | bytes accessed | tf_op | source)
XLA Modules:
  0.0 64.3 jit_solution(2833589961133619428)
XLA Ops:
  0.0 0.0 copy-start
  0.0 0.0 copy-start.2
  0.0 0.0 copy-start.3
  0.0 0.9 %slice_select_fusion = f32[32,384]{1,0:T(8,128)S(1)} fusion(f32[32,16384]{1,0:T(8,128)} %x_hbm.1, s32[32,64]{1,0:T(8,128)} %valid_ref.1, pred[384]{0:T(512)(128)(4,1)S(1)} %iota_compare_fusion), kind=kLoop, calls=%fused_computation | loop fusion | flops 24576 | bytes 106880 | tf_op jit(solution)/shard_map/jit(_where)/select_n | solution.py:217
  0.9 2.2 %collective-permute-start = (f32[32,384]{1,0:T(8,128)S(1)}, f32[32,384]{1,0:T(8,128)S(1)}, u32[]{:S(2)}, u32[]{:S(2)}) collective-permute-start(f32[32,384]{1,0:T(8,128)S(1)} %slice_select_fusion), channel_id=1, source_target_pairs={{0,1},{1,2},{2,3},{3,4},{4,5},{5,6},{6,7},{7,0},{8,9},{9,10},{10,1... | collective-permute-start | bytes 147464 | tf_op jit(solution)/shard_map/ppermute | solution.py:218
  3.1 4.1 %spectra.1 = (f32[2304,128]{1,0:T(8,128)S(1)}, f32[2304,128]{1,0:T(8,128)S(1)}, f32[32,384]{1,0:T(8,128)S(1)}) custom-call(f32[32,16384]{1,0:T(8,128)} %x_hbm.1, bf16[5,256,256]{2,1,0:T(8,128)(2,1)} %constant.8.clone.table_hbm.table_ref), custom_call_target="tpu_custom_call" | custom-call | tf_op jit(solution)/shard_map/spectra/pallas_call | solution.py:147
  7.1 0.0 collective-permute-done.before_ref
  7.2 0.0 copy-done
  7.2 0.0 copy-done.2
  7.2 0.0 copy-done.3
  7.2 1.3 %turn.1 = bf16[128,32,128]{2,1,0:T(8,128)(2,1)S(1)} custom-call(f32[2304,128]{1,0:T(8,128)S(1)} %get-tuple-element.8.re_ref, f32[2304,128]{1,0:T(8,128)S(1)} %get-tuple-element.9.im_ref, f32[32,384]{1,0:T(8,128)S(1)} %get-tuple-element.10.head_ref, f32[32,384]{1,0:T(8,128)S(1)} %collective-permute-done.before_ref, s32[1,32]{1,0:T(1,128)S(1)} %bitcast.5, ...), custom_call_target="tpu_custom_call" | custom-call | tf_op jit(solution)/shard_map/turn/pallas_call | solution.py:202
  8.5 29.3 %all_to_all.10 = bf16[128,32,128]{2,1,0:T(8,128)(2,1)S(1)} all-to-all(bf16[128,32,128]{2,1,0:T(8,128)(2,1)S(1)} %turn.1), channel_id=1, replica_groups=mesh['chan'=16,'tm'=8] {'chan','tm'}, dimensions={0} | all-to-all | bytes 2097152 | tf_op jit(solution)/shard_map/all_to_all | solution.py:328
  37.8 0.0 copy-start.1
  37.8 1.4 %cross_spectra.1 = bf16[16,8,32,128]{3,2,1,0:T(8,128)(2,1)S(1)} custom-call(bf16[16,8,32,128]{3,2,1,0:T(8,128)(2,1)S(1)} %bitcast.3), custom_call_target="tpu_custom_call" | custom-call | tf_op jit(solution)/shard_map/cross_spectra/pallas_call | solution.py:262
  39.2 23.2 %all_to_all.11.back_ref = bf16[128,32,128]{2,1,0:T(8,128)(2,1)S(1)} all-to-all(bf16[128,32,128]{2,1,0:T(8,128)(2,1)S(1)} %bitcast.4), channel_id=1, replica_groups=mesh['chan'=16,'tm'=8] {'chan','tm'}, dimensions={0} | all-to-all | bytes 2097152 | tf_op jit(solution)/shard_map/all_to_all | solution.py:330
  62.4 0.0 copy-done.1
  62.4 1.9 %inverse.1 = f32[32,64,256]{2,1,0:T(8,128)} custom-call(bf16[128,32,128]{2,1,0:T(8,128)(2,1)S(1)} %all_to_all.11.back_ref, bf16[256,640]{1,0:T(8,128)(2,1)S(1)} %copy-done.1), custom_call_target="tpu_custom_call" | custom-call | tf_op jit(solution)/shard_map/inverse/pallas_call | solution.py:310
  (1 shorter events, 0.0 us)
Async XLA Ops:
  0.0 7.2 %copy-start = (bf16[5,256,256]{2,1,0:T(8,128)(2,1)S(1)}, bf16[5,256,256]{2,1,0:T(8,128)(2,1)}, u32[]{:S(2)}) copy-start(bf16[5,256,256]{2,1,0:T(8,128)(2,1)} %constant.8.clone.table_hbm.table_ref) | copy-start | bytes 1966084
  0.0 7.2 %copy-start.2 = (s32[32,64]{1,0:T(8,128)S(1)}, s32[32,64]{1,0:T(8,128)}, u32[]{:S(2)}) copy-start(s32[32,64]{1,0:T(8,128)} %valid_ref.1) | copy-start | bytes 24580
  0.0 7.2 %copy-start.3 = (s32[32]{0:T(128)S(1)}, s32[32]{0:T(128)}, u32[]{:S(2)}) copy-start(s32[32]{0:T(128)} %param.6) | copy-start | bytes 388
  0.9 6.3 %collective-permute-start = (f32[32,384]{1,0:T(8,128)S(1)}, f32[32,384]{1,0:T(8,128)S(1)}, u32[]{:S(2)}, u32[]{:S(2)}) collective-permute-start(f32[32,384]{1,0:T(8,128)S(1)} %slice_select_fusion), channel_id=1, source_target_pairs={{0,1},{1,2},{2,3},{3,4},{4,5},{5,6},{6,7},{7,0},{8,9},{9,10},{10,1... | collective-permute-start | bytes 147464 | tf_op jit(solution)/shard_map/ppermute | solution.py:218
  37.8 24.6 %copy-start.1 = (bf16[256,640]{1,0:T(8,128)(2,1)S(1)}, bf16[256,640]{1,0:T(8,128)(2,1)}, u32[]{:S(2)}) copy-start(bf16[256,640]{1,0:T(8,128)(2,1)} %constant.9.clone.table_ref) | copy-start | bytes 983044

commit v7 on v6

--- a/solution.py
+++ b/solution.py
@@ -15,6 +15,7 @@
 F32 = jnp.float32
 BF16 = jnp.bfloat16
 VMEM = pl.BlockSpec(memory_space=pltpu.VMEM)
+ORDER = np.concatenate([np.arange(0, BINS, 2), np.arange(1, BINS, 2)])
 
 
 def split(table):
@@ -30,16 +31,19 @@
     edge = np.arange(LANES)[:, None]
     edge = np.where(edge < HALF_WIN, SEG_LEN + edge, edge - LANES)
     box_edge = (np.abs(edge - t_out) <= HALF_WIN).astype(BF16)
-    phase = 2.0 * np.pi / SEG_LEN * (t_in * np.arange(BINS)[None, :] % SEG_LEN)
-    forward = np.concatenate([np.cos(phase), -np.sin(phase)], axis=1).astype(np.float32)
-    bins = np.arange(BINS)
-    band = (np.abs(bins[:, None] - bins[None, :]) <= SMOOTH).astype(BF16)
+    phase = 2.0 * np.pi / SEG_LEN * (np.arange(LANES)[:, None] * ORDER[None, :] % SEG_LEN)
+    real, imag = np.cos(phase), -np.sin(phase)
+    half = BINS // 2
+    even = split(np.concatenate([real[:, :half], imag[:, :half]], axis=1).astype(np.float32))
+    odd = split(np.concatenate([imag[:, half:], real[:, half:]], axis=1).astype(np.float32))
+    even, odd = (np.tile(np.concatenate(both, axis=1), (2, 1)) for both in (even, odd))
+    band = (np.abs(ORDER[:, None] - ORDER[None, :]) <= SMOOTH).astype(BF16)
     band = np.concatenate([band, np.ones((BINS, BINS), BF16)], axis=1)
-    return np.stack([box_mid, np.tile(box_edge, (2, 1)), *split(forward), np.tile(band, (2, 1))])
+    return np.stack([box_mid, np.tile(box_edge, (2, 1)), even, odd, np.tile(band, (2, 1))])
 
 
 def inverse_table():
-    freq = np.arange(BINS)[:, None]
+    freq = ORDER[:, None]
     lag = np.arange(SEG_LEN)[None, :] - BINS
     phase = 2.0 * np.pi / SEG_LEN * (freq * lag % SEG_LEN)
     table = np.concatenate([np.cos(phase), -np.sin(phase)], axis=0).astype(np.float32)
@@ -62,13 +66,18 @@
     a_high, a_low = halves(jnp.abs(x))
     e_both = jnp.concatenate(halves(jnp.abs(rim)), axis=1)
     total = mxu(a_high, mid) + mxu(a_low, mid) + mxu(e_both, edge)
-    return halves(x / (total * (1.0 / (2 * HALF_WIN + 1)) + 1e-05))
-
-
-def transform(high, low, table_ref):
-    table = table_ref[2]
-    spec = mxu(high, table) + mxu(low, table) + mxu(high, table_ref[3])
-    re, im = spec[:, :BINS], spec[:, BINS:]
+    normed = x / (total * (1.0 / (2 * HALF_WIN + 1)) + 1e-05)
+    head, tail = normed[:, :LANES], normed[:, LANES:]
+    return [jnp.concatenate(halves(part), axis=1) for part in (head + tail, head - tail)]
+
+
+def transform(sums, differences, table_ref):
+    even, odd = mxu(sums, table_ref[2]), mxu(differences, table_ref[3])
+    even = even[:, :LANES] + even[:, LANES:]
+    odd = odd[:, :LANES] + odd[:, LANES:]
+    front = lax.broadcasted_iota(jnp.int32, even.shape, 1) < BINS // 2
+    re = jnp.where(front, even, odd)
+    im = pltpu.roll(jnp.where(front, odd, even), BINS // 2, 1)
     return re, im, jnp.concatenate(halves(re * re + im * im), axis=1)
 
 
@@ -279,12 +288,21 @@
 def inverse_kernel(back_ref, table_ref, out_hbm, turned_ref, out_ref, sems):
     _, rows, lanes = back_ref.shape
     cols = lanes // 2
-    for f in range(BINS):
-        turned_ref[f * (rows + PAD) : f * (rows + PAD) + rows, :] = back_ref[f].astype(F32)
+    part = rows // 2
+
+    def place(first, bins):
+        for f in bins:
+            at = f * (rows + PAD) + first
+            turned_ref[at : at + part, :] = back_ref[f, first : first + part].astype(F32)
+
+    place(0, range(BINS))
     groups = rows // ROWS
+    step = BINS // (groups // 2)
     pieces = {}
     copies = []
     for g in range(groups + 1):
+        if g < groups // 2:
+            place(part, range(g * step, (g + 1) * step))
         if g < groups:
             piece = []
             for i in range(g * ROWS, (g + 1) * ROWS):

time: 64.5 us -> 64.4 us (level)
  no operation moved by 1% of the time
where the time goes in v7:
time: 64.4 us; the launch traced here: 64.2 us
  blocking collectives  52.5 us (82%)
  Pallas kernels  8.57 us (13%)
  starting transfers between devices  2.19 us (3%)
  other arithmetic  0.88 us (1%)
    all_to_all x1, blocking collectives, body(): got = lax.all_to_all(sent, ALL, 0, 0, tiled=True)  29.3 us
    all_to_all x1, blocking collectives, body(): back = lax.all_to_all(pieces.reshape(got.shape), ALL, 0, 0, tiled=True)  23.2 us
    pallas_call x1, Pallas kernels, spectra(): pl.pallas_call(spectra_kernel, out_shape=(half, half, jax.ShapeDtypeStruc...  3.88 us
    ppermute x1, starting transfers between devices, front(): lax.ppermute(tail, 'tm', [(i, (i + 1) % slabs) for i in range(slabs)])  2.19 us
    pallas_call x1, Pallas kernels, inverse(): pl.pallas_call(inverse_kernel, out_shape=jax.ShapeDtypeStruct(shape, F32)...  1.9 us
    pallas_call x1, Pallas kernels, cross_spectra(): pl.pallas_call(cross_kernel, out_shape=jax.ShapeDtypeStruct(got.shape, BF...  1.4 us
    pallas_call x1, Pallas kernels, turn(): pl.pallas_call(turn_kernel, out_shape=jax.ShapeDtypeStruct((BINS, rows, 2...  1.39 us
  transfers between devices with their start and end apart: 1, of which 0 were waited for; matrix products, arithmetic and copies ran while one was open for 0% of the time, Pallas kernels for 6%

profile of v7, /device:TPU:1, one launch (start us, length us, event | category | flops | bytes accessed | tf_op | source)
XLA Modules:
  0.0 64.2 jit_solution(12317133646826910301)
XLA Ops:
  0.0 0.0 copy-start
  0.0 0.0 copy-start.2
  0.0 0.0 copy-start.3
  0.0 0.9 %slice_select_fusion = f32[32,384]{1,0:T(8,128)S(1)} fusion(f32[32,16384]{1,0:T(8,128)} %x_hbm.1, s32[32,64]{1,0:T(8,128)} %valid_ref.1, pred[384]{0:T(512)(128)(4,1)S(1)} %iota_compare_fusion), kind=kLoop, calls=%fused_computation | loop fusion | flops 24576 | bytes 106880 | tf_op jit(solution)/shard_map/jit(_where)/select_n | solution.py:226
  0.9 2.2 %collective-permute-start = (f32[32,384]{1,0:T(8,128)S(1)}, f32[32,384]{1,0:T(8,128)S(1)}, u32[]{:S(2)}, u32[]{:S(2)}) collective-permute-start(f32[32,384]{1,0:T(8,128)S(1)} %slice_select_fusion), channel_id=1, source_target_pairs={{0,1},{1,2},{2,3},{3,4},{4,5},{5,6},{6,7},{7,0},{8,9},{9,10},{10,1... | collective-permute-start | bytes 147464 | tf_op jit(solution)/shard_map/ppermute | solution.py:227
  3.1 3.9 %spectra.1 = (f32[2304,128]{1,0:T(8,128)S(1)}, f32[2304,128]{1,0:T(8,128)S(1)}, f32[32,384]{1,0:T(8,128)S(1)}) custom-call(f32[32,16384]{1,0:T(8,128)} %x_hbm.1, bf16[5,256,256]{2,1,0:T(8,128)(2,1)} %constant.8.clone.table_hbm.table_ref), custom_call_target="tpu_custom_call" | custom-call | tf_op jit(solution)/shard_map/spectra/pallas_call | solution.py:156
  7.0 0.0 collective-permute-done.before_ref
  7.0 0.0 copy-done
  7.0 0.0 copy-done.2
  7.0 0.0 copy-done.3
  7.0 1.4 %turn.1 = bf16[128,32,128]{2,1,0:T(8,128)(2,1)S(1)} custom-call(f32[2304,128]{1,0:T(8,128)S(1)} %get-tuple-element.8.re_ref, f32[2304,128]{1,0:T(8,128)S(1)} %get-tuple-element.9.im_ref, f32[32,384]{1,0:T(8,128)S(1)} %get-tuple-element.10.head_ref, f32[32,384]{1,0:T(8,128)S(1)} %collective-permute-done.before_ref, s32[1,32]{1,0:T(1,128)S(1)} %bitcast.5, ...), custom_call_target="tpu_custom_call" | custom-call | tf_op jit(solution)/shard_map/turn/pallas_call | solution.py:211
  8.4 29.3 %all_to_all.10 = bf16[128,32,128]{2,1,0:T(8,128)(2,1)S(1)} all-to-all(bf16[128,32,128]{2,1,0:T(8,128)(2,1)S(1)} %turn.1), channel_id=1, replica_groups=mesh['chan'=16,'tm'=8] {'chan','tm'}, dimensions={0} | all-to-all | bytes 2097152 | tf_op jit(solution)/shard_map/all_to_all | solution.py:346
  37.7 0.0 copy-start.1
  37.7 1.4 %cross_spectra.1 = bf16[16,8,32,128]{3,2,1,0:T(8,128)(2,1)S(1)} custom-call(bf16[16,8,32,128]{3,2,1,0:T(8,128)(2,1)S(1)} %bitcast.3), custom_call_target="tpu_custom_call" | custom-call | tf_op jit(solution)/shard_map/cross_spectra/pallas_call | solution.py:271
  39.1 23.2 %all_to_all.11.back_ref = bf16[128,32,128]{2,1,0:T(8,128)(2,1)S(1)} all-to-all(bf16[128,32,128]{2,1,0:T(8,128)(2,1)S(1)} %bitcast.4), channel_id=1, replica_groups=mesh['chan'=16,'tm'=8] {'chan','tm'}, dimensions={0} | all-to-all | bytes 2097152 | tf_op jit(solution)/shard_map/all_to_all | solution.py:348
  62.3 0.0 copy-done.1
  62.3 1.9 %inverse.1 = f32[32,64,256]{2,1,0:T(8,128)} custom-call(bf16[128,32,128]{2,1,0:T(8,128)(2,1)S(1)} %all_to_all.11.back_ref, bf16[256,640]{1,0:T(8,128)(2,1)S(1)} %copy-done.1), custom_call_target="tpu_custom_call" | custom-call | tf_op jit(solution)/shard_map/inverse/pallas_call | solution.py:328
  (1 shorter events, 0.0 us)
Async XLA Ops:
  0.0 7.0 %copy-start = (bf16[5,256,256]{2,1,0:T(8,128)(2,1)S(1)}, bf16[5,256,256]{2,1,0:T(8,128)(2,1)}, u32[]{:S(2)}) copy-start(bf16[5,256,256]{2,1,0:T(8,128)(2,1)} %constant.8.clone.table_hbm.table_ref) | copy-start | bytes 1966084
  0.0 7.0 %copy-start.2 = (s32[32,64]{1,0:T(8,128)S(1)}, s32[32,64]{1,0:T(8,128)}, u32[]{:S(2)}) copy-start(s32[32,64]{1,0:T(8,128)} %valid_ref.1) | copy-start | bytes 24580
  0.0 7.0 %copy-start.3 = (s32[32]{0:T(128)S(1)}, s32[32]{0:T(128)}, u32[]{:S(2)}) copy-start(s32[32]{0:T(128)} %param.6) | copy-start | bytes 388
  0.9 6.1 %collective-permute-start = (f32[32,384]{1,0:T(8,128)S(1)}, f32[32,384]{1,0:T(8,128)S(1)}, u32[]{:S(2)}, u32[]{:S(2)}) collective-permute-start(f32[32,384]{1,0:T(8,128)S(1)} %slice_select_fusion), channel_id=1, source_target_pairs={{0,1},{1,2},{2,3},{3,4},{4,5},{5,6},{6,7},{7,0},{8,9},{9,10},{10,1... | collective-permute-start | bytes 147464 | tf_op jit(solution)/shard_map/ppermute | solution.py:227
  37.7 24.6 %copy-start.1 = (bf16[256,640]{1,0:T(8,128)(2,1)S(1)}, bf16[256,640]{1,0:T(8,128)(2,1)}, u32[]{:S(2)}) copy-start(bf16[256,640]{1,0:T(8,128)(2,1)} %constant.9.clone.table_ref) | copy-start | bytes 983044

commit v8 on v7

--- a/solution.py
+++ b/solution.py
@@ -85,8 +85,7 @@
     sums = mxu(power, table_ref[4])
     floor = sums[:, :BINS] * (1.0 / (2 * SMOOTH + 1)) + sums[:, BINS:] * (0.1 / BINS)
     scale = lax.rsqrt(floor + 1e-06)
-    first = lax.broadcasted_iota(jnp.int32, re.shape, 1) == 0
-    return jnp.where(first, 1.0, re * scale), jnp.where(first, 0.0, im * scale)
+    return re * scale, im * scale
 
 
 def beside(right, left):
@@ -95,12 +94,28 @@
 
 
 GROUP = 8
-PIECES = 4
+PIECES = 8
 PAD = 4
 END = SEG_LEN + LANES
-
-
-def spectra_kernel(x_hbm, table_hbm, re_ref, im_ref, head_ref, x_ref, table_ref, sems):
+LATE = 16
+
+
+def gather(ref, firsts):
+    own = [ref[:, i : i + SEG_LEN] for i in firsts]
+    rim = [
+        beside(ref[:, i + SEG_LEN : i + SEG_LEN + LANES], ref[:, i - LANES : i]) for i in firsts
+    ]
+    return jnp.concatenate(own, axis=0), jnp.concatenate(rim, axis=0)
+
+
+def keep(parts, refs, slot, rows):
+    for part, ref in zip(parts, refs):
+        for s in range(part.shape[0] // rows):
+            first = (slot + s) * (rows + PAD)
+            ref[first : first + rows, :] = part[s * rows : (s + 1) * rows]
+
+
+def spectra_kernel(x_hbm, table_hbm, re_ref, im_ref, head_ref, rest_ref, x_ref, table_ref, sems):
     rows, span = x_ref.shape
     segs = span // SEG_LEN
     width = span // PIECES
@@ -112,56 +127,50 @@
         )
         for g in range(PIECES)
     ]
-    table_copy = pltpu.make_async_copy(table_hbm, table_ref, sems.at[PIECES])
-    copies[0].start()
-    table_copy.start()
-    for copy in copies[1:]:
+    box, others = (
+        pltpu.make_async_copy(table_hbm.at[at], table_ref.at[at], sems.at[PIECES + i])
+        for i, at in enumerate((slice(0, 2), slice(2, 5)))
+    )
+    needed = (GROUP + 1) * SEG_LEN + LANES
+    early = -(-needed // width)
+    for copy in (*copies[:early], box, *copies[early:], others):
         copy.start()
-    arrived = 0
-    table_copy.wait()
-    starts = list(range(1, segs - 1, GROUP))
+    for copy in (*copies[:early], box):
+        copy.wait()
+    stop = segs - 1 - LATE
+    starts = list(range(1, stop, GROUP))
     normed, spec = {}, {}
     for g in range(len(starts) + 2):
         if g < len(starts):
-            own, rim = [], []
-            stop = min(starts[g] + GROUP, segs - 1)
-            while arrived * width < stop * SEG_LEN + LANES:
-                for copy in copies[arrived : arrived + 2]:
+            if g == 1:
+                for copy in (*copies[early:], others):
                     copy.wait()
-                arrived += 2
-            for s in range(starts[g], stop):
-                first, last = s * SEG_LEN, (s + 1) * SEG_LEN
-                own.append(x_ref[:, first:last])
-                rim.append(
-                    beside(x_ref[:, last : last + LANES], x_ref[:, first - LANES : first])
-                )
-            normed[g] = level(
-                jnp.concatenate(own, axis=0), jnp.concatenate(rim, axis=0), table_ref
-            )
+            firsts = [s * SEG_LEN for s in range(starts[g], min(starts[g] + GROUP, stop))]
+            normed[g] = level(*gather(x_ref, firsts), table_ref)
         if 0 <= g - 1 < len(starts):
             spec[g - 1] = transform(*normed.pop(g - 1), table_ref)
         if 0 <= g - 2:
-            re, im = whiten(*spec.pop(g - 2), table_ref)
-            for s in range(re.shape[0] // rows):
-                first = (starts[g - 2] + 1 + s) * (rows + PAD)
-                re_ref[first : first + rows, :] = re[s * rows : (s + 1) * rows]
-                im_ref[first : first + rows, :] = im[s * rows : (s + 1) * rows]
+            done = whiten(*spec.pop(g - 2), table_ref)
+            keep(done, (re_ref, im_ref), starts[g - 2] + 1, rows)
     head_ref[...] = x_ref[:, :END]
+    rest_ref[...] = x_ref[:, stop * SEG_LEN - LANES : (segs - 1) * SEG_LEN + LANES]
 
 
 def spectra(traces, table):
     rows, span = traces.shape
     segs = span // SEG_LEN
-    half = jax.ShapeDtypeStruct((segs * (rows + PAD), BINS), F32)
+    half = jax.ShapeDtypeStruct(((segs - LATE) * (rows + PAD), BINS), F32)
+    head = jax.ShapeDtypeStruct((rows, END), F32)
+    rest = jax.ShapeDtypeStruct((rows, LATE * SEG_LEN + 2 * LANES), F32)
     return pl.pallas_call(
         spectra_kernel,
-        out_shape=(half, half, jax.ShapeDtypeStruct((rows, END), F32)),
+        out_shape=(half, half, head, rest),
         in_specs=[pl.BlockSpec(memory_space=pltpu.HBM)] * 2,
-        out_specs=(VMEM, VMEM, VMEM),
+        out_specs=(VMEM,) * 4,
         scratch_shapes=[
             pltpu.VMEM(traces.shape, F32),
             pltpu.VMEM(table.shape, BF16),
-            pltpu.SemaphoreType.DMA((PIECES + 1,)),
+            pltpu.SemaphoreType.DMA((PIECES + 2,)),
         ],
         compiler_params=pltpu.CompilerParams(vmem_limit_bytes=32 << 20),
         name="spectra",
@@ -172,7 +181,8 @@
 
 
 def turn_kernel(
-    re_ref, im_ref, head_ref, before_ref, live_ref, valid_ref, table_ref, out_ref, turned_ref
+    re_ref, im_ref, head_ref, rest_ref, before_ref, live_ref, valid_ref, table_ref,
+    out_ref, turned_ref, late_re_ref, late_im_ref,
 ):
     rows = head_ref.shape[0]
     segs = valid_ref.shape[1]
@@ -182,15 +192,23 @@
         beside(head_ref[:, :LANES] * joined, before_ref[:, :LANES]),
         beside(head_ref[:, SEG_LEN:END], before_ref[:, SEG_LEN:END] * joined),
     ]
-    fixed = level(x, jnp.concatenate(rim, axis=0), table_ref)
-    fixed = whiten(*transform(*fixed, table_ref), table_ref)
+    groups = [(x, jnp.concatenate(rim, axis=0))]
+    for g in range(0, LATE, GROUP):
+        firsts = [LANES + s * SEG_LEN for s in range(g, g + GROUP)]
+        groups.append(gather(rest_ref, firsts))
+    groups = [level(*group, table_ref) for group in groups]
+    groups = [transform(*group, table_ref) for group in groups]
+    fixed, *late = [whiten(*group, table_ref) for group in groups]
+    for g, done in enumerate(late):
+        keep(done, (late_re_ref, late_im_ref), g * GROUP, rows)
     row = lax.broadcasted_iota(jnp.int32, (8, BINS), 0)
     for c in range(rows):
         pieces = []
-        for ref, ends in zip((re_ref, im_ref), fixed):
-            picked = ref[pl.ds(c, segs, stride=rows + PAD), :]
+        for ref, late_ref, ends in zip((re_ref, im_ref), (late_re_ref, late_im_ref), fixed):
+            picked = ref[pl.ds(c, segs - LATE, stride=rows + PAD), :]
+            late = late_ref[pl.ds(c, LATE, stride=rows + PAD), :]
             top = jnp.where(row == 1, ends[rows + c : rows + c + 1], picked[:8])
-            pieces += [jnp.where(row == 0, ends[c : c + 1], top), picked[8:]]
+            pieces += [jnp.where(row == 0, ends[c : c + 1], top), picked[8:], late]
         turned_ref[pl.ds(c, BINS, stride=rows + PAD), :] = jnp.concatenate(pieces, axis=0).T
     live = jnp.broadcast_to(live_ref[...].astype(F32), (rows, rows))
     here = [lax.broadcasted_iota(jnp.int32, (rows, rows), axis) for axis in range(2)]
@@ -201,7 +219,8 @@
     other = before_ref[:, :LANES]
     other = jnp.where(lane < segs, other, pltpu.roll(other, segs, 1))
     mask = live * pltpu.roll(jnp.where(lane % segs == segs - 1, other, valid), 1, 1)
-    for f in range(BINS):
+    out_ref[0] = jnp.where(lane < segs, mask, 0.0).astype(BF16)
+    for f in range(1, BINS):
         first = f * (rows + PAD)
         out_ref[f] = (turned_ref[first : first + rows, :] * mask).astype(BF16)
 
@@ -211,9 +230,13 @@
     return pl.pallas_call(
         turn_kernel,
         out_shape=jax.ShapeDtypeStruct((BINS, rows, 2 * segs), BF16),
-        in_specs=[VMEM] * 7,
+        in_specs=[VMEM] * 8,
         out_specs=VMEM,
-        scratch_shapes=[pltpu.VMEM((BINS * (rows + PAD), LANES), F32)],
+        scratch_shapes=[
+            pltpu.VMEM((BINS * (rows + PAD), LANES), F32),
+            pltpu.VMEM((LATE * (rows + PAD), BINS), F32),
+            pltpu.VMEM((LATE * (rows + PAD), BINS), F32),
+        ],
         compiler_params=pltpu.CompilerParams(vmem_limit_bytes=32 << 20),
         name="turn",
     )(*parts, before, live[None, :], valid, table)

time: 64.4 us -> 64.1 us (level)
  transfers between devices with their start and end apart: 1 -> 1, of which waited for: 0 -> 1; matrix products, arithmetic and copies ran while one was open for 0% -> 0% of each run, Pallas kernels for 6% -> 5%
where the time goes in v8:
time: 64.1 us; the launch traced here: 63.9 us
  blocking collectives  52 us (81%)
  Pallas kernels  8.26 us (13%)
  starting transfers between devices  2.19 us (3%)
  other arithmetic  0.88 us (1%)
    all_to_all x1, blocking collectives, body(): got = lax.all_to_all(sent, ALL, 0, 0, tiled=True)  28.8 us
    all_to_all x1, blocking collectives, body(): back = lax.all_to_all(pieces.reshape(got.shape), ALL, 0, 0, tiled=True)  23.2 us
    pallas_call x1, Pallas kernels, spectra(): pl.pallas_call(spectra_kernel, out_shape=(half, half, head, rest), in_spe...  3.32 us
    ppermute x1, starting transfers between devices, front(): lax.ppermute(tail, 'tm', [(i, (i + 1) % slabs) for i in range(slabs)])  2.19 us
    pallas_call x1, Pallas kernels, inverse(): pl.pallas_call(inverse_kernel, out_shape=jax.ShapeDtypeStruct(shape, F32)...  1.9 us
    pallas_call x1, Pallas kernels, turn(): pl.pallas_call(turn_kernel, out_shape=jax.ShapeDtypeStruct((BINS, rows, 2...  1.63 us
    pallas_call x1, Pallas kernels, cross_spectra(): pl.pallas_call(cross_kernel, out_shape=jax.ShapeDtypeStruct(got.shape, BF...  1.4 us
  transfers between devices with their start and end apart: 1, of which 1 were waited for; matrix products, arithmetic and copies ran while one was open for 0% of the time, Pallas kernels for 5%

profile of v8, /device:TPU:1, one launch (start us, length us, event | category | flops | bytes accessed | tf_op | source)
XLA Modules:
  0.0 63.9 jit_solution(9701426038236779604)
XLA Ops:
  0.0 0.0 copy-start
  0.0 0.0 copy-start.2
  0.0 0.0 copy-start.3
  0.0 0.9 %slice_select_fusion = f32[32,384]{1,0:T(8,128)S(1)} fusion(f32[32,16384]{1,0:T(8,128)} %x_hbm.1, s32[32,64]{1,0:T(8,128)} %valid_ref.1, pred[384]{0:T(512)(128)(4,1)S(1)} %iota_compare_fusion), kind=kLoop, calls=%fused_computation | loop fusion | flops 24576 | bytes 106880 | tf_op jit(solution)/shard_map/jit(_where)/select_n | solution.py:249
  0.9 2.2 %collective-permute-start = (f32[32,384]{1,0:T(8,128)S(1)}, f32[32,384]{1,0:T(8,128)S(1)}, u32[]{:S(2)}, u32[]{:S(2)}) collective-permute-start(f32[32,384]{1,0:T(8,128)S(1)} %slice_select_fusion), channel_id=1, source_target_pairs={{0,1},{1,2},{2,3},{3,4},{4,5},{5,6},{6,7},{7,0},{8,9},{9,10},{10,1... | collective-permute-start | bytes 147464 | tf_op jit(solution)/shard_map/ppermute | solution.py:250
  3.1 3.3 %spectra.1 = (f32[1728,128]{1,0:T(8,128)S(1)}, f32[1728,128]{1,0:T(8,128)S(1)}, f32[32,384]{1,0:T(8,128)S(1)}, f32[32,4352]{1,0:T(8,128)S(1)}) custom-call(f32[32,16384]{1,0:T(8,128)} %x_hbm.1, bf16[5,256,256]{2,1,0:T(8,128)(2,1)} %constant.8.clone.table_hbm.table_ref), custom_call_target="tpu_custom_call" | custom-call | tf_op jit(solution)/shard_map/spectra/pallas_call | solution.py:165
  6.4 0.5 collective-permute-done.before_ref
  6.9 0.0 copy-done
  6.9 0.0 copy-done.2
  6.9 0.0 copy-done.3
  6.9 1.6 %turn.1 = bf16[128,32,128]{2,1,0:T(8,128)(2,1)S(1)} custom-call(f32[1728,128]{1,0:T(8,128)S(1)} %get-tuple-element.9.re_ref, f32[1728,128]{1,0:T(8,128)S(1)} %get-tuple-element.10.im_ref, f32[32,384]{1,0:T(8,128)S(1)} %get-tuple-element.11.head_ref, f32[32,4352]{1,0:T(8,128)S(1)} %get-tuple-element.12.rest_ref, ...), custom_call_target="tpu_custom_call" | custom-call | tf_op jit(solution)/shard_map/turn/pallas_call | solution.py:230
  8.6 28.8 %all_to_all.10 = bf16[128,32,128]{2,1,0:T(8,128)(2,1)S(1)} all-to-all(bf16[128,32,128]{2,1,0:T(8,128)(2,1)S(1)} %turn.1), channel_id=1, replica_groups=mesh['chan'=16,'tm'=8] {'chan','tm'}, dimensions={0} | all-to-all | bytes 2097152 | tf_op jit(solution)/shard_map/all_to_all | solution.py:369
  37.4 0.0 copy-start.1
  37.4 1.4 %cross_spectra.1 = bf16[16,8,32,128]{3,2,1,0:T(8,128)(2,1)S(1)} custom-call(bf16[16,8,32,128]{3,2,1,0:T(8,128)(2,1)S(1)} %bitcast.3), custom_call_target="tpu_custom_call" | custom-call | tf_op jit(solution)/shard_map/cross_spectra/pallas_call | solution.py:294
  38.8 23.2 %all_to_all.11.back_ref = bf16[128,32,128]{2,1,0:T(8,128)(2,1)S(1)} all-to-all(bf16[128,32,128]{2,1,0:T(8,128)(2,1)S(1)} %bitcast.4), channel_id=1, replica_groups=mesh['chan'=16,'tm'=8] {'chan','tm'}, dimensions={0} | all-to-all | bytes 2097152 | tf_op jit(solution)/shard_map/all_to_all | solution.py:371
  62.0 0.0 copy-done.1
  62.0 1.9 %inverse.1 = f32[32,64,256]{2,1,0:T(8,128)} custom-call(bf16[128,32,128]{2,1,0:T(8,128)(2,1)S(1)} %all_to_all.11.back_ref, bf16[256,640]{1,0:T(8,128)(2,1)S(1)} %copy-done.1), custom_call_target="tpu_custom_call" | custom-call | tf_op jit(solution)/shard_map/inverse/pallas_call | solution.py:351
  (1 shorter events, 0.0 us)
Async XLA Ops:
  0.0 6.9 %copy-start = (bf16[5,256,256]{2,1,0:T(8,128)(2,1)S(1)}, bf16[5,256,256]{2,1,0:T(8,128)(2,1)}, u32[]{:S(2)}) copy-start(bf16[5,256,256]{2,1,0:T(8,128)(2,1)} %constant.8.clone.table_hbm.table_ref) | copy-start | bytes 1966084
  0.0 6.9 %copy-start.2 = (s32[32,64]{1,0:T(8,128)S(1)}, s32[32,64]{1,0:T(8,128)}, u32[]{:S(2)}) copy-start(s32[32,64]{1,0:T(8,128)} %valid_ref.1) | copy-start | bytes 24580
  0.0 6.9 %copy-start.3 = (s32[32]{0:T(128)S(1)}, s32[32]{0:T(128)}, u32[]{:S(2)}) copy-start(s32[32]{0:T(128)} %param.6) | copy-start | bytes 388
  0.9 6.0 %collective-permute-start = (f32[32,384]{1,0:T(8,128)S(1)}, f32[32,384]{1,0:T(8,128)S(1)}, u32[]{:S(2)}, u32[]{:S(2)}) collective-permute-start(f32[32,384]{1,0:T(8,128)S(1)} %slice_select_fusion), channel_id=1, source_target_pairs={{0,1},{1,2},{2,3},{3,4},{4,5},{5,6},{6,7},{7,0},{8,9},{9,10},{10,1... | collective-permute-start | bytes 147464 | tf_op jit(solution)/shard_map/ppermute | solution.py:250
  37.4 24.6 %copy-start.1 = (bf16[256,640]{1,0:T(8,128)(2,1)S(1)}, bf16[256,640]{1,0:T(8,128)(2,1)}, u32[]{:S(2)}) copy-start(bf16[256,640]{1,0:T(8,128)(2,1)} %constant.9.clone.table_ref) | copy-start | bytes 983044

commit v9 on v8

--- a/solution.py
+++ b/solution.py
@@ -36,10 +36,10 @@
     half = BINS // 2
     even = split(np.concatenate([real[:, :half], imag[:, :half]], axis=1).astype(np.float32))
     odd = split(np.concatenate([imag[:, half:], real[:, half:]], axis=1).astype(np.float32))
-    even, odd = (np.tile(np.concatenate(both, axis=1), (2, 1)) for both in (even, odd))
+    even, odd = (np.concatenate(both, axis=1) for both in (even, odd))
     band = (np.abs(ORDER[:, None] - ORDER[None, :]) <= SMOOTH).astype(BF16)
     band = np.concatenate([band, np.ones((BINS, BINS), BF16)], axis=1)
-    return np.stack([box_mid, np.tile(box_edge, (2, 1)), even, odd, np.tile(band, (2, 1))])
+    return np.concatenate([box_mid, box_edge, even, odd, band], axis=0)
 
 
 def inverse_table():
@@ -61,8 +61,13 @@
     return high, (x - high.astype(F32)).astype(BF16)
 
 
+def twice(table_ref, block):
+    table = table_ref[block * LANES : (block + 1) * LANES, :]
+    return jnp.concatenate([table, table], axis=0)
+
+
 def level(x, rim, table_ref):
-    mid, edge = table_ref[0], table_ref[1]
+    mid, edge = table_ref[: 2 * LANES, :], twice(table_ref, 2)
     a_high, a_low = halves(jnp.abs(x))
     e_both = jnp.concatenate(halves(jnp.abs(rim)), axis=1)
     total = mxu(a_high, mid) + mxu(a_low, mid) + mxu(e_both, edge)
@@ -72,7 +77,7 @@
 
 
 def transform(sums, differences, table_ref):
-    even, odd = mxu(sums, table_ref[2]), mxu(differences, table_ref[3])
+    even, odd = mxu(sums, twice(table_ref, 3)), mxu(differences, twice(table_ref, 4))
     even = even[:, :LANES] + even[:, LANES:]
     odd = odd[:, :LANES] + odd[:, LANES:]
     front = lax.broadcasted_iota(jnp.int32, even.shape, 1) < BINS // 2
@@ -82,7 +87,7 @@
 
 
 def whiten(re, im, power, table_ref):
-    sums = mxu(power, table_ref[4])
+    sums = mxu(power, twice(table_ref, 5))
     floor = sums[:, :BINS] * (1.0 / (2 * SMOOTH + 1)) + sums[:, BINS:] * (0.1 / BINS)
     scale = lax.rsqrt(floor + 1e-06)
     return re * scale, im * scale
@@ -129,7 +134,7 @@
     ]
     box, others = (
         pltpu.make_async_copy(table_hbm.at[at], table_ref.at[at], sems.at[PIECES + i])
-        for i, at in enumerate((slice(0, 2), slice(2, 5)))
+        for i, at in enumerate((slice(0, 3 * LANES), slice(3 * LANES, 6 * LANES)))
     )
     needed = (GROUP + 1) * SEG_LEN + LANES
     early = -(-needed // width)

time: 64.1 us -> 64 us (level)
  no operation moved by 1% of the time
where the time goes in v9:
time: 64 us; the launch traced here: 63.8 us
  blocking collectives  51.9 us (81%)
  Pallas kernels  8.17 us (13%)
  starting transfers between devices  2.19 us (3%)
  other arithmetic  0.87 us (1%)
    all_to_all x1, blocking collectives, body(): got = lax.all_to_all(sent, ALL, 0, 0, tiled=True)  28.7 us
    all_to_all x1, blocking collectives, body(): back = lax.all_to_all(pieces.reshape(got.shape), ALL, 0, 0, tiled=True)  23.2 us
    pallas_call x1, Pallas kernels, spectra(): pl.pallas_call(spectra_kernel, out_shape=(half, half, head, rest), in_spe...  3.23 us
    ppermute x1, starting transfers between devices, front(): lax.ppermute(tail, 'tm', [(i, (i + 1) % slabs) for i in range(slabs)])  2.19 us
    pallas_call x1, Pallas kernels, inverse(): pl.pallas_call(inverse_kernel, out_shape=jax.ShapeDtypeStruct(shape, F32)...  1.9 us
    pallas_call x1, Pallas kernels, turn(): pl.pallas_call(turn_kernel, out_shape=jax.ShapeDtypeStruct((BINS, rows, 2...  1.64 us
    pallas_call x1, Pallas kernels, cross_spectra(): pl.pallas_call(cross_kernel, out_shape=jax.ShapeDtypeStruct(got.shape, BF...  1.4 us
  transfers between devices with their start and end apart: 1, of which 1 were waited for; matrix products, arithmetic and copies ran while one was open for 0% of the time, Pallas kernels for 5%

profile of v9, /device:TPU:1, one launch (start us, length us, event | category | flops | bytes accessed | tf_op | source)
XLA Modules:
  0.0 63.8 jit_solution(10314967560337287614)
XLA Ops:
  0.0 0.0 copy-start
  0.0 0.0 copy-start.2
  0.0 0.0 copy-start.3
  0.0 0.9 %slice_select_fusion = f32[32,384]{1,0:T(8,128)S(1)} fusion(f32[32,16384]{1,0:T(8,128)} %x_hbm.1, s32[32,64]{1,0:T(8,128)} %valid_ref.1, pred[384]{0:T(512)(128)(4,1)S(1)} %iota_compare_fusion), kind=kLoop, calls=%fused_computation | loop fusion | flops 24576 | bytes 106880 | tf_op jit(solution)/shard_map/jit(_where)/select_n | solution.py:254
  0.9 2.2 %collective-permute-start = (f32[32,384]{1,0:T(8,128)S(1)}, f32[32,384]{1,0:T(8,128)S(1)}, u32[]{:S(2)}, u32[]{:S(2)}) collective-permute-start(f32[32,384]{1,0:T(8,128)S(1)} %slice_select_fusion), channel_id=1, source_target_pairs={{0,1},{1,2},{2,3},{3,4},{4,5},{5,6},{6,7},{7,0},{8,9},{9,10},{10,1... | collective-permute-start | bytes 147464 | tf_op jit(solution)/shard_map/ppermute | solution.py:255
  3.1 3.2 %spectra.1 = (f32[1728,128]{1,0:T(8,128)S(1)}, f32[1728,128]{1,0:T(8,128)S(1)}, f32[32,384]{1,0:T(8,128)S(1)}, f32[32,4352]{1,0:T(8,128)S(1)}) custom-call(f32[32,16384]{1,0:T(8,128)} %x_hbm.1, bf16[768,256]{1,0:T(8,128)(2,1)} %constant.8.clone.table_hbm.table_ref), custom_call_target="tpu_custom_call" | custom-call | tf_op jit(solution)/shard_map/spectra/pallas_call | solution.py:170
  6.3 0.6 collective-permute-done.before_ref
  6.9 0.0 copy-done
  6.9 0.0 copy-done.2
  6.9 0.0 copy-done.3
  6.9 1.6 %turn.1 = bf16[128,32,128]{2,1,0:T(8,128)(2,1)S(1)} custom-call(f32[1728,128]{1,0:T(8,128)S(1)} %get-tuple-element.9.re_ref, f32[1728,128]{1,0:T(8,128)S(1)} %get-tuple-element.10.im_ref, f32[32,384]{1,0:T(8,128)S(1)} %get-tuple-element.11.head_ref, f32[32,4352]{1,0:T(8,128)S(1)} %get-tuple-element.12.rest_ref, ...), custom_call_target="tpu_custom_call" | custom-call | tf_op jit(solution)/shard_map/turn/pallas_call | solution.py:235
  8.6 28.7 %all_to_all.10 = bf16[128,32,128]{2,1,0:T(8,128)(2,1)S(1)} all-to-all(bf16[128,32,128]{2,1,0:T(8,128)(2,1)S(1)} %turn.1), channel_id=1, replica_groups=mesh['chan'=16,'tm'=8] {'chan','tm'}, dimensions={0} | all-to-all | bytes 2097152 | tf_op jit(solution)/shard_map/all_to_all | solution.py:374
  37.3 0.0 copy-start.1
  37.3 1.4 %cross_spectra.1 = bf16[16,8,32,128]{3,2,1,0:T(8,128)(2,1)S(1)} custom-call(bf16[16,8,32,128]{3,2,1,0:T(8,128)(2,1)S(1)} %bitcast.3), custom_call_target="tpu_custom_call" | custom-call | tf_op jit(solution)/shard_map/cross_spectra/pallas_call | solution.py:299
  38.7 23.2 %all_to_all.11.back_ref = bf16[128,32,128]{2,1,0:T(8,128)(2,1)S(1)} all-to-all(bf16[128,32,128]{2,1,0:T(8,128)(2,1)S(1)} %bitcast.4), channel_id=1, replica_groups=mesh['chan'=16,'tm'=8] {'chan','tm'}, dimensions={0} | all-to-all | bytes 2097152 | tf_op jit(solution)/shard_map/all_to_all | solution.py:376
  61.9 0.0 copy-done.1
  61.9 1.9 %inverse.1 = f32[32,64,256]{2,1,0:T(8,128)} custom-call(bf16[128,32,128]{2,1,0:T(8,128)(2,1)S(1)} %all_to_all.11.back_ref, bf16[256,640]{1,0:T(8,128)(2,1)S(1)} %copy-done.1), custom_call_target="tpu_custom_call" | custom-call | tf_op jit(solution)/shard_map/inverse/pallas_call | solution.py:356
  (1 shorter events, 0.0 us)
Async XLA Ops:
  0.0 6.9 %copy-start = (bf16[768,256]{1,0:T(8,128)(2,1)S(1)}, bf16[768,256]{1,0:T(8,128)(2,1)}, u32[]{:S(2)}) copy-start(bf16[768,256]{1,0:T(8,128)(2,1)} %constant.8.clone.table_hbm.table_ref) | copy-start | bytes 1179652
  0.0 6.9 %copy-start.2 = (s32[32,64]{1,0:T(8,128)S(1)}, s32[32,64]{1,0:T(8,128)}, u32[]{:S(2)}) copy-start(s32[32,64]{1,0:T(8,128)} %valid_ref.1) | copy-start | bytes 24580
  0.0 6.9 %copy-start.3 = (s32[32]{0:T(128)S(1)}, s32[32]{0:T(128)}, u32[]{:S(2)}) copy-start(s32[32]{0:T(128)} %param.6) | copy-start | bytes 388
  0.9 6.0 %collective-permute-start = (f32[32,384]{1,0:T(8,128)S(1)}, f32[32,384]{1,0:T(8,128)S(1)}, u32[]{:S(2)}, u32[]{:S(2)}) collective-permute-start(f32[32,384]{1,0:T(8,128)S(1)} %slice_select_fusion), channel_id=1, source_target_pairs={{0,1},{1,2},{2,3},{3,4},{4,5},{5,6},{6,7},{7,0},{8,9},{9,10},{10,1... | collective-permute-start | bytes 147464 | tf_op jit(solution)/shard_map/ppermute | solution.py:255
  37.3 24.6 %copy-start.1 = (bf16[256,640]{1,0:T(8,128)(2,1)S(1)}, bf16[256,640]{1,0:T(8,128)(2,1)}, u32[]{:S(2)}) copy-start(bf16[256,640]{1,0:T(8,128)(2,1)} %constant.9.clone.table_ref) | copy-start | bytes 983044

commit v10 on v9

--- a/solution.py
+++ b/solution.py
@@ -132,15 +132,18 @@
         )
         for g in range(PIECES)
     ]
-    box, others = (
-        pltpu.make_async_copy(table_hbm.at[at], table_ref.at[at], sems.at[PIECES + i])
-        for i, at in enumerate((slice(0, 3 * LANES), slice(3 * LANES, 6 * LANES)))
+    others = pltpu.make_async_copy(
+        table_hbm.at[3 * LANES :], table_ref.at[3 * LANES :], sems.at[PIECES]
     )
     needed = (GROUP + 1) * SEG_LEN + LANES
     early = -(-needed // width)
-    for copy in (*copies[:early], box, *copies[early:], others):
+    for copy in (*copies, others):
         copy.start()
-    for copy in (*copies[:early], box):
+    row = lax.broadcasted_iota(jnp.int32, (3 * LANES, SEG_LEN), 0)
+    col = lax.broadcasted_iota(jnp.int32, (3 * LANES, SEG_LEN), 1)
+    sample = jnp.where(row < SEG_LEN + HALF_WIN, row, row - (SEG_LEN + LANES))
+    table_ref[: 3 * LANES, :] = jnp.where(jnp.abs(sample - col) <= HALF_WIN, 1.0, 0.0).astype(BF16)
+    for copy in copies[:early]:
         copy.wait()
     stop = segs - 1 - LATE
     starts = list(range(1, stop, GROUP))
@@ -175,7 +178,7 @@
         scratch_shapes=[
             pltpu.VMEM(traces.shape, F32),
             pltpu.VMEM(table.shape, BF16),
-            pltpu.SemaphoreType.DMA((PIECES + 2,)),
+            pltpu.SemaphoreType.DMA((PIECES + 1,)),
         ],
         compiler_params=pltpu.CompilerParams(vmem_limit_bytes=32 << 20),
         name="spectra",

time: 64 us -> 63.9 us (level)
  no operation moved by 1% of the time
where the time goes in v10:
time: 63.9 us; the launch traced here: 63.7 us
  blocking collectives  51.8 us (81%)
  Pallas kernels  8.11 us (13%)
  starting transfers between devices  2.19 us (3%)
  other arithmetic  0.87 us (1%)
  waiting for transfers between devices  0.67 us (1%)
    all_to_all x1, blocking collectives, body(): got = lax.all_to_all(sent, ALL, 0, 0, tiled=True)  28.6 us
    all_to_all x1, blocking collectives, body(): back = lax.all_to_all(pieces.reshape(got.shape), ALL, 0, 0, tiled=True)  23.2 us
    pallas_call x1, Pallas kernels, spectra(): pl.pallas_call(spectra_kernel, out_shape=(half, half, head, rest), in_spe...  3.17 us
    ppermute x1, starting transfers between devices, front(): lax.ppermute(tail, 'tm', [(i, (i + 1) % slabs) for i in range(slabs)])  2.19 us
    pallas_call x1, Pallas kernels, inverse(): pl.pallas_call(inverse_kernel, out_shape=jax.ShapeDtypeStruct(shape, F32)...  1.9 us
    pallas_call x1, Pallas kernels, turn(): pl.pallas_call(turn_kernel, out_shape=jax.ShapeDtypeStruct((BINS, rows, 2...  1.64 us
    pallas_call x1, Pallas kernels, cross_spectra(): pl.pallas_call(cross_kernel, out_shape=jax.ShapeDtypeStruct(got.shape, BF...  1.4 us
  transfers between devices with their start and end apart: 1, of which 1 were waited for; matrix products, arithmetic and copies ran while one was open for 0% of the time, Pallas kernels for 5%

profile of v10, /device:TPU:1, one launch (start us, length us, event | category | flops | bytes accessed | tf_op | source)
XLA Modules:
  0.0 63.7 jit_solution(3840028552176940297)
XLA Ops:
  0.0 0.0 copy-start
  0.0 0.0 copy-start.2
  0.0 0.0 copy-start.3
  0.0 0.9 %slice_select_fusion = f32[32,384]{1,0:T(8,128)S(1)} fusion(f32[32,16384]{1,0:T(8,128)} %x_hbm.1, s32[32,64]{1,0:T(8,128)} %valid_ref.1, pred[384]{0:T(512)(128)(4,1)S(1)} %iota_compare_fusion), kind=kLoop, calls=%fused_computation | loop fusion | flops 24576 | bytes 106880 | tf_op jit(solution)/shard_map/jit(_where)/select_n | solution.py:257
  0.9 2.2 %collective-permute-start = (f32[32,384]{1,0:T(8,128)S(1)}, f32[32,384]{1,0:T(8,128)S(1)}, u32[]{:S(2)}, u32[]{:S(2)}) collective-permute-start(f32[32,384]{1,0:T(8,128)S(1)} %slice_select_fusion), channel_id=1, source_target_pairs={{0,1},{1,2},{2,3},{3,4},{4,5},{5,6},{6,7},{7,0},{8,9},{9,10},{10,1... | collective-permute-start | bytes 147464 | tf_op jit(solution)/shard_map/ppermute | solution.py:258
  3.1 3.2 %spectra.1 = (f32[1728,128]{1,0:T(8,128)S(1)}, f32[1728,128]{1,0:T(8,128)S(1)}, f32[32,384]{1,0:T(8,128)S(1)}, f32[32,4352]{1,0:T(8,128)S(1)}) custom-call(f32[32,16384]{1,0:T(8,128)} %x_hbm.1, bf16[768,256]{1,0:T(8,128)(2,1)} %constant.8.clone.table_hbm.table_ref), custom_call_target="tpu_custom_call" | custom-call | tf_op jit(solution)/shard_map/spectra/pallas_call | solution.py:173
  6.2 0.7 %collective-permute-done.before_ref = f32[32,384]{1,0:T(8,128)S(1)} collective-permute-done((f32[32,384]{1,0:T(8,128)S(1)}, f32[32,384]{1,0:T(8,128)S(1)}, u32[]{:S(2)}, u32[]{:S(2)}) %collective-permute-start) | collective-permute-done | bytes 49184 | tf_op jit(solution)/shard_map/ppermute | solution.py:258
  6.9 0.0 copy-done
  6.9 0.0 copy-done.2
  6.9 0.0 copy-done.3
  6.9 1.6 %turn.1 = bf16[128,32,128]{2,1,0:T(8,128)(2,1)S(1)} custom-call(f32[1728,128]{1,0:T(8,128)S(1)} %get-tuple-element.9.re_ref, f32[1728,128]{1,0:T(8,128)S(1)} %get-tuple-element.10.im_ref, f32[32,384]{1,0:T(8,128)S(1)} %get-tuple-element.11.head_ref, f32[32,4352]{1,0:T(8,128)S(1)} %get-tuple-element.12.rest_ref, ...), custom_call_target="tpu_custom_call" | custom-call | tf_op jit(solution)/shard_map/turn/pallas_call | solution.py:238
  8.6 28.6 %all_to_all.10 = bf16[128,32,128]{2,1,0:T(8,128)(2,1)S(1)} all-to-all(bf16[128,32,128]{2,1,0:T(8,128)(2,1)S(1)} %turn.1), channel_id=1, replica_groups=mesh['chan'=16,'tm'=8] {'chan','tm'}, dimensions={0} | all-to-all | bytes 2097152 | tf_op jit(solution)/shard_map/all_to_all | solution.py:377
  37.2 0.0 copy-start.1
  37.2 1.4 %cross_spectra.1 = bf16[16,8,32,128]{3,2,1,0:T(8,128)(2,1)S(1)} custom-call(bf16[16,8,32,128]{3,2,1,0:T(8,128)(2,1)S(1)} %bitcast.3), custom_call_target="tpu_custom_call" | custom-call | tf_op jit(solution)/shard_map/cross_spectra/pallas_call | solution.py:302
  38.6 23.2 %all_to_all.11.back_ref = bf16[128,32,128]{2,1,0:T(8,128)(2,1)S(1)} all-to-all(bf16[128,32,128]{2,1,0:T(8,128)(2,1)S(1)} %bitcast.4), channel_id=1, replica_groups=mesh['chan'=16,'tm'=8] {'chan','tm'}, dimensions={0} | all-to-all | bytes 2097152 | tf_op jit(solution)/shard_map/all_to_all | solution.py:379
  61.8 0.0 copy-done.1
  61.8 1.9 %inverse.1 = f32[32,64,256]{2,1,0:T(8,128)} custom-call(bf16[128,32,128]{2,1,0:T(8,128)(2,1)S(1)} %all_to_all.11.back_ref, bf16[256,640]{1,0:T(8,128)(2,1)S(1)} %copy-done.1), custom_call_target="tpu_custom_call" | custom-call | tf_op jit(solution)/shard_map/inverse/pallas_call | solution.py:359
  (1 shorter events, 0.0 us)
Async XLA Ops:
  0.0 6.9 %copy-start = (bf16[768,256]{1,0:T(8,128)(2,1)S(1)}, bf16[768,256]{1,0:T(8,128)(2,1)}, u32[]{:S(2)}) copy-start(bf16[768,256]{1,0:T(8,128)(2,1)} %constant.8.clone.table_hbm.table_ref) | copy-start | bytes 1179652
  0.0 6.9 %copy-start.2 = (s32[32,64]{1,0:T(8,128)S(1)}, s32[32,64]{1,0:T(8,128)}, u32[]{:S(2)}) copy-start(s32[32,64]{1,0:T(8,128)} %valid_ref.1) | copy-start | bytes 24580
  0.0 6.9 %copy-start.3 = (s32[32]{0:T(128)S(1)}, s32[32]{0:T(128)}, u32[]{:S(2)}) copy-start(s32[32]{0:T(128)} %param.6) | copy-start | bytes 388
  0.9 6.0 %collective-permute-start = (f32[32,384]{1,0:T(8,128)S(1)}, f32[32,384]{1,0:T(8,128)S(1)}, u32[]{:S(2)}, u32[]{:S(2)}) collective-permute-start(f32[32,384]{1,0:T(8,128)S(1)} %slice_select_fusion), channel_id=1, source_target_pairs={{0,1},{1,2},{2,3},{3,4},{4,5},{5,6},{6,7},{7,0},{8,9},{9,10},{10,1... | collective-permute-start | bytes 147464 | tf_op jit(solution)/shard_map/ppermute | solution.py:258
  37.2 24.6 %copy-start.1 = (bf16[256,640]{1,0:T(8,128)(2,1)S(1)}, bf16[256,640]{1,0:T(8,128)(2,1)}, u32[]{:S(2)}) copy-start(bf16[256,640]{1,0:T(8,128)(2,1)} %constant.9.clone.table_ref) | copy-start | bytes 983044
